TPU v7x, 32 devices: a whole 2x2x4 slice. The times are simulated.
32 devices in a mesh: dp: 16 (over z, y, x), seq: 2 (over core).
Axes of the slice: x: 2, y: 2, z: 4, core: 2. Of those that a mesh axis runs over, the one named last changes fastest.
Arguments:
- layer_input: bfloat16 [64, 512, 768], P('dp', 'seq'), may hold values from -24 to 24, as said below
- segment_ids: int32 [64, 512], P('dp'), may hold values from 0 to 3, never falling along the last dimension, each value on 1 to 256 neighbouring positions
- cotangent: bfloat16 [64, 512, 768], P('dp', 'seq'), may hold values from -6 to 6
- heads_weight: float32 [768, 2304], P(('dp', 'seq')), may hold values from -0.21875 to 0.21875
- heads_first: float32 [768, 2304], P(('dp', 'seq')), may hold values from -0.00024414062 to 0.00024414062
- heads_second: float32 [768, 2304], P(('dp', 'seq')), may hold values from 1.4128508e-10 to 5.651403e-10
- merge_weight: float32 [768, 768], P(('dp', 'seq')), may hold values from -0.625 to 0.625
- merge_first: float32 [768, 768], P(('dp', 'seq')), may hold values from -0.00024414062 to 0.00024414062
- merge_second: float32 [768, 768], P(('dp', 'seq')), may hold values from 1.4128508e-10 to 5.651403e-10
- expand_weight: float32 [768, 3072], P(('dp', 'seq')), may hold values from -0.21875 to 0.21875
- expand_first: float32 [768, 3072], P(('dp', 'seq')), may hold values from -0.00024414062 to 0.00024414062
- expand_second: float32 [768, 3072], P(('dp', 'seq')), may hold values from 1.4128508e-10 to 5.651403e-10
- shrink_weight: float32 [3072, 768], P(('dp', 'seq')), may hold values from -0.109375 to 0.109375
- shrink_first: float32 [3072, 768], P(('dp', 'seq')), may hold values from -0.00024414062 to 0.00024414062
- shrink_second: float32 [3072, 768], P(('dp', 'seq')), may hold values from 1.4128508e-10 to 5.651403e-10
- norm_gains: float32 [768, 2], P(('dp', 'seq')), may hold values from 0.25 to 2.7, as said below
- gains_first: float32 [768, 2], P(('dp', 'seq')), may hold values from -0.0007324219 to 0.0007324219
- gains_second: float32 [768, 2], P(('dp', 'seq')), may hold values from 1.2715657e-09 to 5.086263e-09
- branch_bias: float32 [768, 6], P(('dp', 'seq')), may hold values from -0.6 to 0.6
- branch_first: float32 [768, 6], P(('dp', 'seq')), may hold values from -0.0007324219 to 0.0007324219
- branch_second: float32 [768, 6], P(('dp', 'seq')), may hold values from 1.2715657e-09 to 5.086263e-09
- hidden_bias: float32 [3072], P(('dp', 'seq')), may hold values from -0.6 to 0.6
- hidden_first: float32 [3072], P(('dp', 'seq')), may hold values from -0.00024414062 to 0.00024414062
- hidden_second: float32 [3072], P(('dp', 'seq')), may hold values from 1.4128508e-10 to 5.651403e-10
Outputs:
- layer_output: bfloat16 [64, 512, 768], P('dp', 'seq')
- input_gradient: float32 [64, 512, 768], P('dp', 'seq')
- gradient_norm: float32 [], replicated
- heads_updated: float32 [768, 2304], P(('dp', 'seq'))
- heads_moment: float32 [768, 2304], P(('dp', 'seq'))
- heads_square: float32 [768, 2304], P(('dp', 'seq'))
- merge_updated: float32 [768, 768], P(('dp', 'seq'))
- merge_moment: float32 [768, 768], P(('dp', 'seq'))
- merge_square: float32 [768, 768], P(('dp', 'seq'))
- expand_updated: float32 [768, 3072], P(('dp', 'seq'))
- expand_moment: float32 [768, 3072], P(('dp', 'seq'))
- expand_square: float32 [768, 3072], P(('dp', 'seq'))
- shrink_updated: float32 [3072, 768], P(('dp', 'seq'))
- shrink_moment: float32 [3072, 768], P(('dp', 'seq'))
- shrink_square: float32 [3072, 768], P(('dp', 'seq'))
- gains_updated: float32 [768, 2], P(('dp', 'seq'))
- gains_moment: float32 [768, 2], P(('dp', 'seq'))
- gains_square: float32 [768, 2], P(('dp', 'seq'))
- branch_updated: float32 [768, 6], P(('dp', 'seq'))
- branch_moment: float32 [768, 6], P(('dp', 'seq'))
- branch_square: float32 [768, 6], P(('dp', 'seq'))
- hidden_updated: float32 [3072], P(('dp', 'seq'))
- hidden_moment: float32 [3072], P(('dp', 'seq'))
- hidden_square: float32 [3072], P(('dp', 'seq'))
- heads_copy: bfloat16 [768, 2304], P(('dp', 'seq'))
- merge_copy: bfloat16 [768, 768], P(('dp', 'seq'))
- expand_copy: bfloat16 [768, 3072], P(('dp', 'seq'))
- shrink_copy: bfloat16 [3072, 768], P(('dp', 'seq'))
Inputs may be any that keep to these rules, and one draw needn't show every extreme that they name: `segment_ids`: along each row the segment numbers never fall and every one of them appears; each segment holds 1 to 256 tokens, and one segment holds exactly 256. `layer_input`: activations of order one. `norm_gains`: positive gains.
All inputs are finite; a program needn't handle non-finite values.
Results may differ from a plain program's by a relative error of at most 0.014.
The roundings to bfloat16 on the way count: a program that leaves them out, or rounds other values in their place, can miss the bound.
Values may be sent and summed in bfloat16 or wider, within the bound.
A program may use at most 192 MiB of HBM per device.

v0:
```python
import jax
import jax.numpy as jnp
from jax import lax
from jax.sharding import PartitionSpec as P

D = 768
HEAD_DIM = 64
STEP = 5


norm_epsilon = 1e-12
masked_score = -1e30
root_half = 0.7071067811865476
inv_root_tau = 0.3989422804014327
clip_limit = 1.0
decay_first = 0.9
decay_second = 0.999
adam_epsilon = 1e-08
weight_decay = 0.01
rate_matrix = 0.05
rate_vector = 0.5


def normalize(hidden):
    center = hidden - jnp.mean(hidden, axis=-1, keepdims=True)
    inverse_scale = lax.rsqrt(jnp.mean(center * center, axis=-1, keepdims=True) + norm_epsilon)
    return (center * inverse_scale, inverse_scale)


def norm_back(upstream, normed, inverse_scale):
    mean_upstream = jnp.mean(upstream, axis=-1, keepdims=True)
    mean_cross = jnp.mean(upstream * normed, axis=-1, keepdims=True)
    return inverse_scale * (upstream - mean_upstream - normed * mean_cross)


def gelu_value(inputs):
    return 0.5 * inputs * (1.0 + lax.erf(inputs * root_half))


def gelu_slope(inputs):
    return (
        0.5 * (1.0 + lax.erf(inputs * root_half))
        + inputs * jnp.exp(-0.5 * inputs * inputs) * inv_root_tau
    )


def cross_rows(operand_left, operand_right):
    return lax.dot_general(
        operand_left, operand_right, (((0,), (0,)), ((), ())), preferred_element_type=jnp.float32
    )


def cross_cols(operand_left, operand_right):
    return lax.dot_general(
        operand_left, operand_right, (((1,), (1,)), ((), ())), preferred_element_type=jnp.float32
    )


def split_heads(matrix):
    return matrix.reshape(matrix.shape[0], matrix.shape[1] // HEAD_DIM, HEAD_DIM)


def masked_scores(query_heads, key_heads, seg_query, seg_key):
    scores = jnp.einsum(
        "qhd,khd->hqk", query_heads, key_heads, preferred_element_type=jnp.float32
    ) * HEAD_DIM ** (-0.5)
    allowed = seg_query[:, None] == seg_key[None, :]
    return jnp.where(allowed[None], scores, masked_score)


def attend_row(row_items):
    query_row, key_row, value_row, seg_query, seg_key = row_items
    masked = masked_scores(split_heads(query_row), split_heads(key_row), seg_query, seg_key)
    row_peak = jnp.max(masked, axis=-1, keepdims=True)
    unscaled = jnp.exp(masked - row_peak)
    denominator = jnp.sum(unscaled, axis=-1, keepdims=True)
    softmax_low = (unscaled / denominator).astype(jnp.bfloat16)
    context = jnp.einsum(
        "hqk,khd->qhd", softmax_low, split_heads(value_row), preferred_element_type=jnp.float32
    )
    return (
        context.reshape(query_row.shape).astype(jnp.bfloat16),
        (row_peak + jnp.log(denominator))[:, :, 0],
    )


def attend_back(row_items):
    query_row, key_row, value_row, seg_query, seg_key, log_total, upstream = row_items
    query_heads = split_heads(query_row)
    key_heads = split_heads(key_row)
    value_heads = split_heads(value_row)
    upstream_heads = split_heads(upstream)
    masked = masked_scores(query_heads, key_heads, seg_query, seg_key)
    softmax_full = jnp.exp(masked - log_total[:, :, None])
    softmax_low = softmax_full.astype(jnp.bfloat16)
    grad_weights = jnp.einsum(
        "qhd,khd->hqk", upstream_heads, value_heads, preferred_element_type=jnp.float32
    )
    grad_value = jnp.einsum(
        "hqk,qhd->khd", softmax_low, upstream_heads, preferred_element_type=jnp.float32
    )
    row_inner = jnp.sum(softmax_full * grad_weights, axis=-1, keepdims=True)
    grad_scores = (softmax_full * (grad_weights - row_inner)).astype(jnp.bfloat16)
    grad_query = jnp.einsum(
        "hqk,khd->qhd", grad_scores, key_heads, preferred_element_type=jnp.float32
    ) * HEAD_DIM ** (-0.5)
    grad_key = jnp.einsum(
        "hqk,qhd->khd", grad_scores, query_heads, preferred_element_type=jnp.float32
    ) * HEAD_DIM ** (-0.5)
    return (
        grad_query.reshape(query_row.shape),
        grad_key.reshape(key_row.shape),
        grad_value.reshape(key_row.shape),
    )


def adamw(weight, moment, square, gradient, factor, step_rate):
    clipped = gradient * factor
    moment_new = decay_first * moment + (1.0 - decay_first) * clipped
    square_new = decay_second * square + (1.0 - decay_second) * clipped * clipped
    corrected = (
        moment_new
        / (1.0 - decay_first**STEP)
        / (jnp.sqrt(square_new / (1.0 - decay_second**STEP)) + adam_epsilon)
    )
    return (weight - step_rate * (corrected + weight_decay * weight), moment_new, square_new)


def per_device(
    layer_input,
    segment_ids,
    cotangent,
    heads_weight,
    heads_first,
    heads_second,
    merge_weight,
    merge_first,
    merge_second,
    expand_weight,
    expand_first,
    expand_second,
    shrink_weight,
    shrink_first,
    shrink_second,
    norm_gains,
    gains_first,
    gains_second,
    branch_bias,
    branch_first,
    branch_second,
    hidden_bias,
    hidden_first,
    hidden_second,
):
    heads_low, merge_low, expand_low, shrink_low, gains_low, biases_low, hidden_low = (
        lax.all_gather(heads_weight.astype(jnp.bfloat16), ("dp", "seq"), axis=0, tiled=True),
        lax.all_gather(merge_weight.astype(jnp.bfloat16), ("dp", "seq"), axis=0, tiled=True),
        lax.all_gather(expand_weight.astype(jnp.bfloat16), ("dp", "seq"), axis=0, tiled=True),
        lax.all_gather(shrink_weight.astype(jnp.bfloat16), ("dp", "seq"), axis=0, tiled=True),
        lax.all_gather(norm_gains.astype(jnp.bfloat16), ("dp", "seq"), axis=0, tiled=True),
        lax.all_gather(branch_bias.astype(jnp.bfloat16), ("dp", "seq"), axis=0, tiled=True),
        lax.all_gather(hidden_bias.astype(jnp.bfloat16), ("dp", "seq"), axis=0, tiled=True),
    )
    gains_full = gains_low.astype(jnp.float32)
    biases_full = biases_low.astype(jnp.float32)
    hidden_full = hidden_low.astype(jnp.float32)
    row_count, local_length = (layer_input.shape[0], layer_input.shape[1])
    flat_input = layer_input.reshape(-1, D)
    projected = jnp.dot(flat_input, heads_low, preferred_element_type=jnp.float32)
    query_local = (
        (projected[:, :D] + biases_full[:, 0])
        .astype(jnp.bfloat16)
        .reshape(row_count, local_length, D)
    )
    key_local = projected[:, D : 2 * D].astype(jnp.bfloat16).reshape(row_count, local_length, D)
    value_local = (
        (projected[:, 2 * D :] + biases_full[:, 1])
        .astype(jnp.bfloat16)
        .reshape(row_count, local_length, D)
    )
    query_spread, key_spread, value_spread = (
        lax.all_to_all(query_local, "seq", split_axis=2, concat_axis=1, tiled=True),
        lax.all_to_all(key_local, "seq", split_axis=2, concat_axis=1, tiled=True),
        lax.all_to_all(value_local, "seq", split_axis=2, concat_axis=1, tiled=True),
    )
    context_spread, log_total = lax.map(
        attend_row, (query_spread, key_spread, value_spread, segment_ids, segment_ids)
    )
    context_local = lax.all_to_all(context_spread, "seq", split_axis=1, concat_axis=2, tiled=True)
    flat_context = context_local.reshape(-1, D)
    attended = (
        jnp.dot(flat_context, merge_low, preferred_element_type=jnp.float32) + biases_full[:, 2]
    )
    normed_one, inverse_one = normalize(flat_input.astype(jnp.float32) + attended)
    first_low = (normed_one * gains_full[:, 0] + biases_full[:, 3]).astype(jnp.bfloat16)
    pre_active = jnp.dot(first_low, expand_low, preferred_element_type=jnp.float32) + hidden_full
    active_low = gelu_value(pre_active).astype(jnp.bfloat16)
    branch_out = (
        jnp.dot(active_low, shrink_low, preferred_element_type=jnp.float32) + biases_full[:, 4]
    )
    normed_two, inverse_two = normalize(first_low.astype(jnp.float32) + branch_out)
    work_output = (
        (normed_two * gains_full[:, 1] + biases_full[:, 5])
        .astype(jnp.bfloat16)
        .reshape(layer_input.shape)
    )
    upstream = cotangent.reshape(-1, D).astype(jnp.float32)
    grad_gain_two = jnp.sum(upstream * normed_two, axis=0)
    grad_shift_two = jnp.sum(upstream, axis=0)
    grad_second = norm_back(upstream * gains_full[:, 1], normed_two, inverse_two)
    branch_grad = grad_second.astype(jnp.bfloat16)
    grad_shrink = cross_rows(active_low, branch_grad)
    grad_shrink_bias = jnp.sum(branch_grad.astype(jnp.float32), axis=0)
    active_grad = (cross_cols(branch_grad, shrink_low) * gelu_slope(pre_active)).astype(
        jnp.bfloat16
    )
    grad_expand = cross_rows(first_low, active_grad)
    grad_hidden = jnp.sum(active_grad.astype(jnp.float32), axis=0)
    grad_first = grad_second + cross_cols(active_grad, expand_low)
    grad_gain_one = jnp.sum(grad_first * normed_one, axis=0)
    grad_shift_one = jnp.sum(grad_first, axis=0)
    grad_sum_one = norm_back(grad_first * gains_full[:, 0], normed_one, inverse_one)
    attended_grad = grad_sum_one.astype(jnp.bfloat16)
    grad_merge = cross_rows(flat_context, attended_grad)
    grad_merge_bias = jnp.sum(attended_grad.astype(jnp.float32), axis=0)
    context_grad = (
        cross_cols(attended_grad, merge_low)
        .astype(jnp.bfloat16)
        .reshape(row_count, local_length, D)
    )
    context_grad_spread = lax.all_to_all(
        context_grad, "seq", split_axis=2, concat_axis=1, tiled=True
    )
    grad_query, grad_key, grad_value = lax.map(
        attend_back,
        (
            query_spread,
            key_spread,
            value_spread,
            segment_ids,
            segment_ids,
            log_total,
            context_grad_spread,
        ),
    )
    query_back, key_back, value_back = (
        lax.all_to_all(
            grad_query.astype(jnp.bfloat16), "seq", split_axis=1, concat_axis=2, tiled=True
        ),
        lax.all_to_all(
            grad_key.astype(jnp.bfloat16), "seq", split_axis=1, concat_axis=2, tiled=True
        ),
        lax.all_to_all(
            grad_value.astype(jnp.bfloat16), "seq", split_axis=1, concat_axis=2, tiled=True
        ),
    )
    projection_grad = jnp.concatenate((query_back, key_back, value_back), axis=2).reshape(-1, 3 * D)
    grad_heads = cross_rows(flat_input, projection_grad)
    work_gradient = (grad_sum_one + cross_cols(projection_grad, heads_low)).reshape(
        layer_input.shape
    )
    grad_query_bias = jnp.sum(query_back.reshape(-1, D).astype(jnp.float32), axis=0)
    grad_value_bias = jnp.sum(value_back.reshape(-1, D).astype(jnp.float32), axis=0)
    grad_gains = jnp.stack((grad_gain_one, grad_gain_two), axis=1)
    grad_biases = jnp.stack(
        (
            grad_query_bias,
            grad_value_bias,
            grad_merge_bias,
            grad_shift_one,
            grad_shrink_bias,
            grad_shift_two,
        ),
        axis=1,
    )
    reduced = (
        lax.psum_scatter(grad_heads, ("dp", "seq"), scatter_dimension=0, tiled=True),
        lax.psum_scatter(grad_merge, ("dp", "seq"), scatter_dimension=0, tiled=True),
        lax.psum_scatter(grad_expand, ("dp", "seq"), scatter_dimension=0, tiled=True),
        lax.psum_scatter(grad_shrink, ("dp", "seq"), scatter_dimension=0, tiled=True),
        lax.psum_scatter(grad_gains, ("dp", "seq"), scatter_dimension=0, tiled=True),
        lax.psum_scatter(grad_biases, ("dp", "seq"), scatter_dimension=0, tiled=True),
        lax.psum_scatter(grad_hidden, ("dp", "seq"), scatter_dimension=0, tiled=True),
    )
    squares_local = sum((jnp.sum(piece * piece) for piece in reduced))
    squares_total = lax.psum(squares_local, ("dp", "seq"))
    gradient_norm = jnp.sqrt(squares_total)
    factor = jnp.minimum(1.0, clip_limit / gradient_norm)
    states = (
        (heads_weight, heads_first, heads_second, rate_matrix),
        (merge_weight, merge_first, merge_second, rate_matrix),
        (expand_weight, expand_first, expand_second, rate_matrix),
        (shrink_weight, shrink_first, shrink_second, rate_matrix),
        (norm_gains, gains_first, gains_second, rate_vector),
        (branch_bias, branch_first, branch_second, rate_vector),
        (hidden_bias, hidden_first, hidden_second, rate_vector),
    )
    results = [
        adamw(state[0], state[1], state[2], gradient, factor, state[3])
        for state, gradient in zip(states, reduced)
    ]
    return (
        work_output,
        work_gradient,
        gradient_norm,
        results[0][0],
        results[0][1],
        results[0][2],
        results[1][0],
        results[1][1],
        results[1][2],
        results[2][0],
        results[2][1],
        results[2][2],
        results[3][0],
        results[3][1],
        results[3][2],
        results[4][0],
        results[4][1],
        results[4][2],
        results[5][0],
        results[5][1],
        results[5][2],
        results[6][0],
        results[6][1],
        results[6][2],
        results[0][0].astype(jnp.bfloat16),
        results[1][0].astype(jnp.bfloat16),
        results[2][0].astype(jnp.bfloat16),
        results[3][0].astype(jnp.bfloat16),
    )


def solution(mesh):
    placed = (
        P("dp", "seq", None),
        P("dp", None),
        P("dp", "seq", None),
        P(("dp", "seq"), None),
        P(("dp", "seq"), None),
        P(("dp", "seq"), None),
        P(("dp", "seq"), None),
        P(("dp", "seq"), None),
        P(("dp", "seq"), None),
        P(("dp", "seq"), None),
        P(("dp", "seq"), None),
        P(("dp", "seq"), None),
        P(("dp", "seq"), None),
        P(("dp", "seq"), None),
        P(("dp", "seq"), None),
        P(("dp", "seq"), None),
        P(("dp", "seq"), None),
        P(("dp", "seq"), None),
        P(("dp", "seq"), None),
        P(("dp", "seq"), None),
        P(("dp", "seq"), None),
        P(("dp", "seq")),
        P(("dp", "seq")),
        P(("dp", "seq")),
    )
    return jax.shard_map(
        per_device,
        mesh=mesh,
        in_specs=placed,
        out_specs=(
            P("dp", "seq", None),
            P("dp", "seq", None),
            P(),
            P(("dp", "seq"), None),
            P(("dp", "seq"), None),
            P(("dp", "seq"), None),
            P(("dp", "seq"), None),
            P(("dp", "seq"), None),
            P(("dp", "seq"), None),
            P(("dp", "seq"), None),
            P(("dp", "seq"), None),
            P(("dp", "seq"), None),
            P(("dp", "seq"), None),
            P(("dp", "seq"), None),
            P(("dp", "seq"), None),
            P(("dp", "seq"), None),
            P(("dp", "seq"), None),
            P(("dp", "seq"), None),
            P(("dp", "seq"), None),
            P(("dp", "seq"), None),
            P(("dp", "seq"), None),
            P(("dp", "seq")),
            P(("dp", "seq")),
            P(("dp", "seq")),
            P(("dp", "seq"), None),
            P(("dp", "seq"), None),
            P(("dp", "seq"), None),
            P(("dp", "seq"), None),
        ),
        check_vma=False,
    )
```

profile of v0, /device:TPU:0, one launch (start us, length us, event | category | flops | bytes accessed | tf_op | source)
XLA Modules:
  0.0 1108.1 jit_solution(547113052117923007)
XLA Ops:
  14.8 43.5 %all-gather = bf16[32,24,6]{1,2,0:T(8,128)(2,1)S(1)} all-gather(bf16[1,24,6]{1,2,0:T(8,128)(2,1)S(1)} %convert_bitcast_fusion), channel_id=1, replica_groups=mesh['dp'=16,'seq'=2] {'dp','seq'}, dimensions={0}, use_global_device_ids=true | all-gather | bytes 9504 | tf_op jit(solution)/shard_map/all_gather | solution.py:161
  59.4 36.7 %all-gather.1 = bf16[32,24,2]{1,2,0:T(2,128)(2,1)S(1)} all-gather(bf16[1,24,2]{1,2,0:T(2,128)(2,1)S(1)} %convert_bitcast_fusion.1), channel_id=1, replica_groups=mesh['dp'=16,'seq'=2] {'dp','seq'}, dimensions={0}, use_global_device_ids=true | all-gather | bytes 3168 | tf_op jit(solution)/shard_map/all_gather | solution.py:160
  97.2 37.2 %all-reduce = bf16[3072]{0:T(1024)(128)(2,1)S(1)} all-reduce(bf16[3072]{0:T(1024)(128)(2,1)S(1)} %dynamic-update-slice), channel_id=1, replica_groups=mesh['dp'=16,'seq'=2] {'dp','seq'}, use_global_device_ids=true, to_apply=%add | all-reduce | flops 3072 | bytes 12288
  178.0 33.1 %while.26 = (s32[]{:T(128)}, bf16[4,512,384]{1,2,0:T(8,128)(2,1)S(1)}, f32[4,6,512]{2,1,0:T(8,128)}, bf16[4,512,384]{1,2,0:T(8,128)(2,1)}, s32[4,512]{1,0:T(4,12...) while((s32[]{:T(128)}, bf16[4,512,384]{1,2,0:T(8,128)(2,1)S(1)}, ...), condition=%wide.region_3.4_spmd, body=%wide.region_0.3_spmd.sunk | while | flops 421983232 | bytes 24750692 | solution.py:186
  225.2 12.6 %multiply_convert_fusion.1 = (bf16[1024,3072]{1,0:T(8,128)(2,1)}, f32[1024,3072]{1,0:T(8,128)}) fusion(f32[3072]{0:T(1024)S(1)} %convert_element_type.150, bf16[768,3072]{1,0:T(8,128)(2,1)} %all-gather.11.cloned.1.call-done, f32[1024,768]{1,0:T(8,128)S(1)} %get-tuple-element.311, f32[768]{0:T(1024)S(1)} %get-tuple-element.219, ...), kind=kOutput, calls=%fused_computation.41 | convolution fusion | flops 4854644736 | bytes 26765312 | tf_op jit(solution)/shard_map/dot_general | solution.py:196
  237.8 24.0 %all-gather.13.cloned.1.call-done = bf16[3072,768]{1,0:T(8,128)(2,1)} async-done(((bf16[96,768]{1,0:T(8,128)(2,1)}), bf16[3072,768]{1,0:T(8,128)(2,1)}) %all-gather.13.cloned.1.call-update) | async-done | bytes 4718608 | tf_op jit(solution)/shard_map/all_gather | solution.py:159
  261.8 8.8 fusion.69
  276.7 14.1 %convert_reduce_fusion = (f32[3072]{0:T(1024)}, bf16[1024,3072]{1,0:T(8,128)(2,1)S(1)}) fusion(f32[1024,3072]{1,0:T(8,128)} %get-tuple-element.313, f32[3072]{0:T(1024)S(1)} %convert_element_type.150, bf16[3072,768]{1,0:T(8,128)(2,1)S(1)} %copy-done.62, f32[1024,768]{1,0:T(8,128)S(1)} %get-tuple-element.288), kind=kOutput, calls=%fused_computation.40 | convolution fusion | flops 4873516032 | bytes 26763264 | tf_op jit(solution)/shard_map/dot_general | solution.py:54
  290.9 6.5 multiply_reduce_fusion.1
  317.2 267.9 %while.27 = (s32[]{:T(128)}, bf16[4,512,384]{2,0,1:T(4,128)(2,1)}, bf16[4,512,384]{2,0,1:T(4,128)(2,1)}, bf16[4,512,384]{2,0,1:T(4,128)(2,1)}, bf16[4,512,384]{1...) while((s32[]{:T(128)}, bf16[4,512,384]{2,0,1:T(4,128)(2,1)}, ...), condition=%wide.region_14.15_spmd, body=%wide.region_12.14_spmd.sunk | while | flops 1031271424 | bytes 100493600 | solution.py:234
  332.1 15.8 %dynamic_update_slice.28 = bf16[4,512,384]{2,0,1:T(4,128)(2,1)} dynamic-update-slice(bf16[4,512,384]{2,0,1:T(4,128)(2,1)} %get-tuple-element.483, bf16[1,512,384]{2,0,1:T(2,128)(2,1)} %copy.219, s32[]{:T(128)} %get-tuple-element.481, s32[]{:T(128)} %constant.52.clone.1..sunk, s32[]{:T(128)} %constant.52.clone.1..sunk) | dynamic-update-slice | bytes 786436 | tf_op jit(solution)/shard_map/while/body/jit(dynamic_update_index_in_dim)/dynamic_update_slice | solution.py:234
  351.8 15.7 %dynamic_update_slice.27 = bf16[4,512,384]{2,0,1:T(4,128)(2,1)} dynamic-update-slice(bf16[4,512,384]{2,0,1:T(4,128)(2,1)} %get-tuple-element.482, bf16[1,512,384]{2,0,1:T(2,128)(2,1)S(1)} %copy.218, s32[]{:T(128)} %get-tuple-element.481, s32[]{:T(128)} %constant.52.clone.1..sunk, s32[]{:T(128)} %constant.52.clone.1..sunk) | dynamic-update-slice | bytes 786436 | tf_op jit(solution)/shard_map/while/body/jit(dynamic_update_index_in_dim)/dynamic_update_slice | solution.py:234
  373.4 9.7 dynamic_update_slice.29
  399.1 15.8 %dynamic_update_slice.28 = bf16[4,512,384]{2,0,1:T(4,128)(2,1)} dynamic-update-slice(bf16[4,512,384]{2,0,1:T(4,128)(2,1)} %get-tuple-element.483, bf16[1,512,384]{2,0,1:T(2,128)(2,1)} %copy.219, s32[]{:T(128)} %get-tuple-element.481, s32[]{:T(128)} %constant.52.clone.1..sunk, s32[]{:T(128)} %constant.52.clone.1..sunk) | dynamic-update-slice | bytes 786436 | tf_op jit(solution)/shard_map/while/body/jit(dynamic_update_index_in_dim)/dynamic_update_slice | solution.py:234
  418.8 15.7 %dynamic_update_slice.27 = bf16[4,512,384]{2,0,1:T(4,128)(2,1)} dynamic-update-slice(bf16[4,512,384]{2,0,1:T(4,128)(2,1)} %get-tuple-element.482, bf16[1,512,384]{2,0,1:T(2,128)(2,1)S(1)} %copy.218, s32[]{:T(128)} %get-tuple-element.481, s32[]{:T(128)} %constant.52.clone.1..sunk, s32[]{:T(128)} %constant.52.clone.1..sunk) | dynamic-update-slice | bytes 786436 | tf_op jit(solution)/shard_map/while/body/jit(dynamic_update_index_in_dim)/dynamic_update_slice | solution.py:234
  440.3 9.7 dynamic_update_slice.29
  466.1 15.7 %dynamic_update_slice.28 = bf16[4,512,384]{2,0,1:T(4,128)(2,1)} dynamic-update-slice(bf16[4,512,384]{2,0,1:T(4,128)(2,1)} %get-tuple-element.483, bf16[1,512,384]{2,0,1:T(2,128)(2,1)} %copy.219, s32[]{:T(128)} %get-tuple-element.481, s32[]{:T(128)} %constant.52.clone.1..sunk, s32[]{:T(128)} %constant.52.clone.1..sunk) | dynamic-update-slice | bytes 786436 | tf_op jit(solution)/shard_map/while/body/jit(dynamic_update_index_in_dim)/dynamic_update_slice | solution.py:234
  485.8 15.7 %dynamic_update_slice.27 = bf16[4,512,384]{2,0,1:T(4,128)(2,1)} dynamic-update-slice(bf16[4,512,384]{2,0,1:T(4,128)(2,1)} %get-tuple-element.482, bf16[1,512,384]{2,0,1:T(2,128)(2,1)S(1)} %copy.218, s32[]{:T(128)} %get-tuple-element.481, s32[]{:T(128)} %constant.52.clone.1..sunk, s32[]{:T(128)} %constant.52.clone.1..sunk) | dynamic-update-slice | bytes 786436 | tf_op jit(solution)/shard_map/while/body/jit(dynamic_update_index_in_dim)/dynamic_update_slice | solution.py:234
  507.3 9.7 dynamic_update_slice.29
  533.0 15.7 %dynamic_update_slice.28 = bf16[4,512,384]{2,0,1:T(4,128)(2,1)} dynamic-update-slice(bf16[4,512,384]{2,0,1:T(4,128)(2,1)} %get-tuple-element.483, bf16[1,512,384]{2,0,1:T(2,128)(2,1)} %copy.219, s32[]{:T(128)} %get-tuple-element.481, s32[]{:T(128)} %constant.52.clone.1..sunk, s32[]{:T(128)} %constant.52.clone.1..sunk) | dynamic-update-slice | bytes 786436 | tf_op jit(solution)/shard_map/while/body/jit(dynamic_update_index_in_dim)/dynamic_update_slice | solution.py:234
  552.7 15.7 %dynamic_update_slice.27 = bf16[4,512,384]{2,0,1:T(4,128)(2,1)} dynamic-update-slice(bf16[4,512,384]{2,0,1:T(4,128)(2,1)} %get-tuple-element.482, bf16[1,512,384]{2,0,1:T(2,128)(2,1)S(1)} %copy.218, s32[]{:T(128)} %get-tuple-element.481, s32[]{:T(128)} %constant.52.clone.1..sunk, s32[]{:T(128)} %constant.52.clone.1..sunk) | dynamic-update-slice | bytes 786436 | tf_op jit(solution)/shard_map/while/body/jit(dynamic_update_index_in_dim)/dynamic_update_slice | solution.py:234
  574.2 9.7 dynamic_update_slice.29
  620.0 9.1 convolution_bitcast_fusion
  629.2 8.0 copy.161
  639.1 11.2 %fusion.70 = f32[768,3072]{1,0:T(8,128)} fusion(bf16[1024,3072]{1,0:T(8,128)(2,1)} %copy-done.16, f32[1024,768]{1,0:T(8,128)S(1)} %copy-done.4, f32[768]{0:T(1024)S(1)} %copy-done.45, f32[768]{0:T(1024)S(1)} %copy-done.41, f32[1024]{0:T(1024)S(1)} %copy-done.37, f32[1024]{0:T(1024)S(1)} %copy-done.32), kind=kOutput, calls=%fused_computation.162 | convolution fusion | flops 4835770368 | bytes 18888704 | tf_op jit(solution)/shard_map/dot_general | solution.py:48
  652.3 10.4 fusion.53
  672.4 41.5 %all-reduce.4 = (f32[768,2]{0,1:T(2,128)S(1)}, f32[768,6]{0,1:T(8,128)S(1)}, f32[3072]{0:T(1024)S(1)}) all-reduce(f32[768,2]{0,1:T(2,128)S(1)} %pad_maximum_fusion, f32[768,6]{0,1:T(8,128)S(1)} %stack.39, f32[3072]{0:T(1024)S(1)} %copy-done.51), channel_id=6, replica_groups=mesh['dp'=16,'seq'=2] {'dp','seq'}, use_global_device_ids=true, to_apply=%region_25.26.clone | all-reduce | flops 9216 | bytes 73728
  717.5 38.0 %reduce-scatter.15.cloned.1.call-done = f32[24,2304]{1,0:T(8,128)} async-done(((f32[768,2304]{1,0:T(8,128)}), f32[24,2304]{1,0:T(8,128)}) %reduce-scatter.15.cloned.1.call-update) | async-done | bytes 221200 | tf_op jit(solution)/shard_map/reduce_scatter | solution.py:277
  759.0 137.6 %reduce-scatter.11.cloned.1.call-done = f32[24,3072]{1,0:T(8,128)} async-done(((f32[768,3072]{1,0:T(8,128)}), f32[24,3072]{1,0:T(8,128)}) %reduce-scatter.11.cloned.1.call-update) | async-done | bytes 294928 | tf_op jit(solution)/shard_map/reduce_scatter | solution.py:279
  898.9 138.8 %reduce-scatter.13.cloned.1.call-done = f32[96,768]{1,0:T(8,128)} async-done(((f32[3072,768]{1,0:T(8,128)}), f32[96,768]{1,0:T(8,128)}) %reduce-scatter.13.cloned.1.call-update) | async-done | bytes 294928 | tf_op jit(solution)/shard_map/reduce_scatter | solution.py:280
  1042.0 9.5 fusion.38
  1051.6 39.7 %psum.7 = f32[]{:T(128)} all-reduce(f32[]{:T(128)S(6)} %add.296), channel_id=1, replica_groups=mesh['dp'=16,'seq'=2] {'dp','seq'}, use_global_device_ids=true, to_apply=%region_38.39 | all-reduce | flops 1 | bytes 8 | tf_op jit(solution)/shard_map/psum | solution.py:286
  (378 shorter events, 293.8 us)
Async XLA Ops:
  7.2 127.2 %copy-start.5 = (bf16[4,256,768]{2,1,0:T(8,128)(2,1)S(1)}, bf16[4,256,768]{2,1,0:T(8,128)(2,1)}, u32[]{:S(2)}) copy-start(bf16[4,256,768]{2,1,0:T(8,128)(2,1)} %param.30) | copy-start | bytes 4718596
  7.2 128.5 %all-gather.7.cloned.1.call-start = ((), (), s32[]{:S(2)}) async-start(), calls=%async_computation.12 | async-start | bytes 3649536 | tf_op jit(solution)/shard_map/all_gather | solution.py:156
  9.0 211.8 %all-gather.9.cloned.1.call-start = ((), (), s32[]{:S(2)}) async-start(), calls=%async_computation.13 | async-start | bytes 1216512 | tf_op jit(solution)/shard_map/all_gather | solution.py:157
  10.6 214.6 %all-gather.11.cloned.1.call-start = ((), (), s32[]{:S(2)}) async-start(), calls=%async_computation.14 | async-start | bytes 4866048 | tf_op jit(solution)/shard_map/all_gather | solution.py:158
  12.3 249.5 %all-gather.13.cloned.1.call-start = ((), (), s32[]{:S(2)}) async-start(), calls=%async_computation.15 | async-start | bytes 4866048 | tf_op jit(solution)/shard_map/all_gather | solution.py:159
  14.0 701.9 %reduce-scatter.9.cloned.1.call-start = ((), (), s32[]{:S(2)}) async-start(), calls=%async_computation.16 | async-start | bytes 2433024 | tf_op jit(solution)/shard_map/reduce_scatter | solution.py:278
  58.7 203.1 %copy-start.44 = (f32[768]{0:T(1024)}, f32[768]{0:T(1024)S(1)}, u32[]{:S(2)}) copy-start(f32[768]{0:T(1024)S(1)} %get-tuple-element.219) | copy-start | bytes 9220
  96.4 201.0 %copy-start.40 = (f32[768]{0:T(1024)}, f32[768]{0:T(1024)S(1)}, u32[]{:S(2)}) copy-start(f32[768]{0:T(1024)S(1)} %get-tuple-element.224) | copy-start | bytes 9220
  224.6 72.8 %copy-start.3 = (f32[1024,768]{1,0:T(8,128)}, f32[1024,768]{1,0:T(8,128)S(1)}, u32[]{:S(2)}) copy-start(f32[1024,768]{1,0:T(8,128)S(1)} %get-tuple-element.311) | copy-start | bytes 9437188
  224.6 72.8 %copy-start.31 = (f32[1024]{0:T(1024)}, f32[1024]{0:T(1024)S(1)}, u32[]{:S(2)}) copy-start(f32[1024]{0:T(1024)S(1)} %broadcast_multiply_fusion.4) | copy-start | bytes 12292
  225.1 72.3 %copy-start.36 = (f32[1024]{0:T(1024)}, f32[1024]{0:T(1024)S(1)}, u32[]{:S(2)}) copy-start(f32[1024]{0:T(1024)S(1)} %add_rsqrt_fusion.1) | copy-start | bytes 12292
  603.6 10.2 all-to-all-start.7
  607.2 148.3 %reduce-scatter.15.cloned.1.call-start = ((), (), s32[]{:S(2)}) async-start(), calls=%async_computation.19 | async-start | bytes 7299072 | tf_op jit(solution)/shard_map/reduce_scatter | solution.py:277
  637.2 259.4 %reduce-scatter.11.cloned.1.call-start = ((), (), s32[]{:S(2)}) async-start(), calls=%async_computation.17 | async-start | bytes 9732096 | tf_op jit(solution)/shard_map/reduce_scatter | solution.py:279
  650.3 387.3 %reduce-scatter.13.cloned.1.call-start = ((), (), s32[]{:S(2)}) async-start(), calls=%async_computation.18 | async-start | bytes 9732096 | tf_op jit(solution)/shard_map/reduce_scatter | solution.py:280
  1041.9 50.1 %copy-start.59 = (f32[96]{0:T(128)S(1)}, f32[96]{0:T(128)}, u32[]{:S(2)}) copy-start(f32[96]{0:T(128)} %param.49) | copy-start | bytes 1156
  1041.9 50.1 %copy-start.60 = (f32[96]{0:T(128)S(1)}, f32[96]{0:T(128)}, u32[]{:S(2)}) copy-start(f32[96]{0:T(128)} %param.50) | copy-start | bytes 1156
  1041.9 50.1 %copy-start.61 = (f32[96]{0:T(128)S(1)}, f32[96]{0:T(128)}, u32[]{:S(2)}) copy-start(f32[96]{0:T(128)} %param.51) | copy-start | bytes 1156
  1041.9 50.7 %copy-start.49 = (f32[24,6]{0,1:T(8,128)S(1)}, f32[24,6]{0,1:T(8,128)}, u32[]{:S(2)}) copy-start(f32[24,6]{0,1:T(8,128)} %param.46) | copy-start | bytes 1732
  1041.9 50.7 %copy-start.54 = (f32[24,6]{0,1:T(8,128)S(1)}, f32[24,6]{0,1:T(8,128)}, u32[]{:S(2)}) copy-start(f32[24,6]{0,1:T(8,128)} %param.47) | copy-start | bytes 1732
  1041.9 50.7 %copy-start.55 = (f32[24,6]{0,1:T(8,128)S(1)}, f32[24,6]{0,1:T(8,128)}, u32[]{:S(2)}) copy-start(f32[24,6]{0,1:T(8,128)} %param.48) | copy-start | bytes 1732
  1041.9 51.4 %copy-start.56 = (f32[24,2]{0,1:T(2,128)S(1)}, f32[24,2]{0,1:T(2,128)}, u32[]{:S(2)}) copy-start(f32[24,2]{0,1:T(2,128)} %param.43) | copy-start | bytes 580
  1042.0 51.4 %copy-start.57 = (f32[24,2]{0,1:T(2,128)S(1)}, f32[24,2]{0,1:T(2,128)}, u32[]{:S(2)}) copy-start(f32[24,2]{0,1:T(2,128)} %param.44) | copy-start | bytes 580
  1042.0 51.4 %copy-start.58 = (f32[24,2]{0,1:T(2,128)S(1)}, f32[24,2]{0,1:T(2,128)}, u32[]{:S(2)}) copy-start(f32[24,2]{0,1:T(2,128)} %param.45) | copy-start | bytes 580
  1042.0 52.0 %copy-start.25 = (f32[96,768]{1,0:T(8,128)S(1)}, f32[96,768]{1,0:T(8,128)}, u32[]{:S(2)}) copy-start(f32[96,768]{1,0:T(8,128)} %param.40) | copy-start | bytes 884740
  1042.0 52.0 %copy-start.28 = (f32[96,768]{1,0:T(8,128)S(1)}, f32[96,768]{1,0:T(8,128)}, u32[]{:S(2)}) copy-start(f32[96,768]{1,0:T(8,128)} %reduce-scatter.13.cloned.1.call-done) | copy-start | bytes 884740
  1042.0 52.0 %copy-start.33 = (f32[96,768]{1,0:T(8,128)S(1)}, f32[96,768]{1,0:T(8,128)}, u32[]{:S(2)}) copy-start(f32[96,768]{1,0:T(8,128)} %param.41) | copy-start | bytes 884740
  1042.0 54.1 %copy-start.26 = (f32[24,3072]{1,0:T(8,128)S(1)}, f32[24,3072]{1,0:T(8,128)}, u32[]{:S(2)}) copy-start(f32[24,3072]{1,0:T(8,128)} %param.37) | copy-start | bytes 884740
  1042.0 54.1 %copy-start.27 = (f32[24,3072]{1,0:T(8,128)S(1)}, f32[24,3072]{1,0:T(8,128)}, u32[]{:S(2)}) copy-start(f32[24,3072]{1,0:T(8,128)} %reduce-scatter.11.cloned.1.call-done) | copy-start | bytes 884740
  1051.5 47.5 %copy-start.29 = (f32[24,2304]{1,0:T(8,128)S(1)}, f32[24,2304]{1,0:T(8,128)}, u32[]{:S(2)}) copy-start(f32[24,2304]{1,0:T(8,128)} %param.31) | copy-start | bytes 663556
  1051.5 47.5 %copy-start.30 = (f32[24,2304]{1,0:T(8,128)S(1)}, f32[24,2304]{1,0:T(8,128)}, u32[]{:S(2)}) copy-start(f32[24,2304]{1,0:T(8,128)} %reduce-scatter.15.cloned.1.call-done) | copy-start | bytes 663556
  1051.5 47.4 %copy-start.38 = (f32[24,2304]{1,0:T(8,128)S(1)}, f32[24,2304]{1,0:T(8,128)}, u32[]{:S(2)}) copy-start(f32[24,2304]{1,0:T(8,128)} %param.32) | copy-start | bytes 663556
  (58 other events, 479.1 us)
Sparse Core Ops, SparseCore 0:
  11.5 62.6 all-gather.6
  77.7 52.7 all-gather.8
  133.9 62.5 all-gather.10
  199.8 61.9 all-gather.12
  317.3 97.9 reduce-scatter.8
  637.3 118.1 reduce-scatter.14
  761.4 135.1 reduce-scatter.10
  902.5 135.1 reduce-scatter.12
where the time goes:
time: 1130 us; the launch traced here: 1110 us
  waiting for transfers between devices  339 us (30%)
  local copies, waits for them, and re-layouts  294 us (26%)
  blocking collectives  236 us (21%)
  matrix products  156 us (14%)
  other arithmetic  57.3 us (5%)
  between operations  21.6 us (2%)
    dynamic_update_slice x24, local copies, waits for them, and re-layouts, per_device(): lax.map(attend_back, (query_spread, key_spread, value_spread, segment_ids...  191 us
    reduce_scatter x1, waiting for transfers between devices, per_device(): lax.psum_scatter(grad_shrink, ('dp', 'seq'), scatter_dimension=0, tiled=T...  139 us
    reduce_scatter x1, waiting for transfers between devices, per_device(): lax.psum_scatter(grad_expand, ('dp', 'seq'), scatter_dimension=0, tiled=T...  138 us
    unnamed x2, blocking collectives  78.7 us
    all_gather x1, blocking collectives, per_device(): lax.all_gather(branch_bias.astype(jnp.bfloat16), ('dp', 'seq'), axis=0, t...  43.5 us
    psum x1, blocking collectives, per_device(): squares_total = lax.psum(squares_local, ('dp', 'seq'))  39.7 us
    reduce_scatter x1, waiting for transfers between devices, per_device(): lax.psum_scatter(grad_heads, ('dp', 'seq'), scatter_dimension=0, tiled=True)  38 us
    all_gather x1, blocking collectives, per_device(): lax.all_gather(norm_gains.astype(jnp.bfloat16), ('dp', 'seq'), axis=0, ti...  36.7 us
  transfers between devices with their start and end apart: 9, of which 4 were waited for; matrix products, arithmetic and copies ran while one was open for 38% of the time, Pallas kernels for 0%

commit v1 on v0

v1 whole, which is shorter than its diff:
```python
import functools

import jax
import jax.numpy as jnp
from jax import lax
from jax.experimental import pallas as pl
from jax.experimental.pallas import tpu as pltpu
from jax.sharding import PartitionSpec as P

D = 768
HEAD_DIM = 64
STEP = 5
MESH = pl.DeviceIdType.MESH

norm_epsilon = 1e-12
masked_score = -1e30
root_half = 0.7071067811865476
inv_root_tau = 0.3989422804014327
clip_limit = 1.0
decay_first = 0.9
decay_second = 0.999
adam_epsilon = 1e-08
weight_decay = 0.01
rate_matrix = 0.05
rate_vector = 0.5


def place():
    chip, core = lax.axis_index("dp"), lax.axis_index("seq")
    return chip // 4, (chip // 2) % 2, chip % 2, core


def device(z, y, x, core):
    return ((z * 2 + y) * 2 + x, core)


def signal(semaphore, target):
    pl.semaphore_signal(semaphore, inc=1, device_id=target, device_id_type=MESH)


def greet(layers, others=()):
    z, y, x, core = place()
    barrier = pltpu.get_barrier_semaphore()
    across = (device(z, y, x, 1 - core), device(z, y, 1 - x, core), device(z, 1 - y, x, core))
    for target in across + tuple(others):
        signal(barrier, target)

    @pl.when(z > 0)
    def _():
        signal(barrier, device(z - 1, y, x, core))

    @pl.when(z < layers - 1)
    def _():
        signal(barrier, device(z + 1, y, x, core))

    beside = jnp.where(z > 0, 1, 0) + jnp.where(z < layers - 1, 1, 0)
    pl.semaphore_wait(barrier, 3 + len(others) + beside)


def remote(source, target, sent, received, to):
    return pltpu.make_async_remote_copy(
        src_ref=source,
        dst_ref=target,
        send_sem=sent,
        recv_sem=received,
        device_id=to,
        device_id_type=MESH,
    )


GATHERED = (
    ("heads", 0, 768, False),
    ("merge", 0, 768, True),
    ("small", 0, 128, True),
    ("heads", 768, 384, True),
    ("shrink", 0, 768, False),
    ("expand", 0, 3072, True),
)


def gather_kernel(
    layers,
    heads_in,
    merge_in,
    expand_in,
    shrink_in,
    small_in,
    tokens_in,
    heads_all,
    merge_all,
    expand_all,
    shrink_all,
    small_all,
    tokens_all,
    heads_block,
    token_room,
    pair_send,
    pair_recv,
    own_sem,
    line_send,
    line_recv,
    first_send,
    first_recv,
    second_send,
    second_recv,
    core_send,
    core_recv,
):
    z, y, x, core = place()
    partner = device(z, y, x, 1 - core)
    own = {"merge": merge_in, "expand": expand_in, "shrink": shrink_in, "small": small_in}
    full = {
        "merge": merge_all,
        "expand": expand_all,
        "shrink": shrink_all,
        "small": small_all,
        "heads": heads_all,
    }
    greet(layers)

    heads_out = remote(
        heads_in.at[1 - core], heads_block.at[core], pair_send.at[0], pair_recv.at[0], partner
    )
    heads_out.start()
    heads_keep = pltpu.make_async_copy(heads_in.at[core], heads_block.at[core], own_sem.at[0])
    heads_keep.start()
    tokens_load = pltpu.make_async_copy(tokens_in, token_room, own_sem.at[1])
    tokens_load.start()

    def own_block(piece):
        name, start, width, _ = GATHERED[piece]
        if name == "heads":
            return heads_block.at[:, :, pl.ds(start, width)]
        return own[name]

    def block(piece, zz, yy, xx, plane):
        name, start, width, _ = GATHERED[piece]
        if name == "heads":
            return full[name].at[zz, yy, xx, :, :, pl.ds(start, width)]
        return full[name].at[zz, yy, xx, plane]

    def couple(piece, zz, plane, moved):
        name, start, width, y_first = GATHERED[piece]
        yy = y if y_first or not moved else 1 - y
        xx = x if not y_first or not moved else 1 - x
        if name == "heads":
            if y_first:
                return full[name].at[zz, :, xx, :, :, pl.ds(start, width)]
            return full[name].at[zz, yy, :, :, :, pl.ds(start, width)]
        if y_first:
            return full[name].at[zz, :, xx, plane]
        return full[name].at[zz, yy, :, plane]

    def across(piece, second):
        y_turn = GATHERED[piece][3] != second
        return device(z, 1 - y, x, core) if y_turn else device(z, y, 1 - x, core)

    def first_block(piece, zz):
        if GATHERED[piece][3]:
            return (zz, 1 - y, x)
        return (zz, y, 1 - x)

    def line_copy(piece, zz, source, target_z):
        return remote(
            source,
            block(piece, zz, y, x, core),
            line_send.at[piece, zz, jnp.where(target_z > z, 0, 1)],
            line_recv.at[piece, zz],
            device(target_z, y, x, core),
        )

    def first_copy(piece, zz, source):
        return remote(
            source,
            block(piece, zz, y, x, core),
            first_send.at[piece, zz],
            first_recv.at[piece, zz],
            across(piece, False),
        )

    def second_copy(piece, zz):
        both = couple(piece, zz, core, False)
        return remote(
            both, both, second_send.at[piece, zz], second_recv.at[piece, zz], across(piece, True)
        )

    def core_copy(piece, zz, stage, source, target):
        return remote(
            source,
            target,
            core_send.at[piece, zz, stage],
            core_recv.at[piece, zz, stage],
            partner,
        )

    def shared(piece):
        return GATHERED[piece][0] != "heads"

    pieces = range(len(GATHERED))
    order = sorted(pieces, key=lambda piece: (GATHERED[piece][0] == "heads", piece))

    def begin(piece):
        mine = own_block(piece)

        @pl.when(z < layers - 1)
        def _():
            line_copy(piece, z, mine, z + 1).start()

        @pl.when(z > 0)
        def _():
            line_copy(piece, z, mine, z - 1).start()

        first_copy(piece, z, mine).start()
        if shared(piece):
            core_copy(piece, z, 0, mine, block(piece, z, y, x, core)).start()
        pltpu.make_async_copy(
            mine, block(piece, z, y, x, core), own_sem.at[2 + piece]
        ).start()

    for piece in order:
        if piece == order[-2]:
            heads_out.wait_recv()
            heads_keep.wait()
        begin(piece)
    tokens_load.wait()
    tokens_out = remote(
        token_room, tokens_all.at[1], pair_send.at[1], pair_recv.at[1], partner
    )
    tokens_out.start()
    tokens_keep = pltpu.make_async_copy(token_room, tokens_all.at[0], own_sem.at[1])
    tokens_keep.start()
    for piece in order:
        pltpu.make_async_copy(
            own_block(piece), block(piece, z, y, x, core), own_sem.at[2 + piece]
        ).wait()

    def arrive_line(piece, zz, below):
        here = block(piece, zz, y, x, core)
        line_copy(piece, zz, here, z).wait_recv()
        if below:

            @pl.when(z < layers - 1)
            def _():
                line_copy(piece, zz, here, z + 1).start()

        else:

            @pl.when(z > 0)
            def _():
                line_copy(piece, zz, here, z - 1).start()

        first_copy(piece, zz, here).start()
        if shared(piece):
            core_copy(piece, zz, 0, here, here).start()

    def arrive_first(piece, zz):
        here = block(piece, *first_block(piece, zz), core)
        remote(
            here, here, first_send.at[piece, zz], first_recv.at[piece, zz], across(piece, False)
        ).wait_recv()
        second_copy(piece, zz).start()
        if shared(piece):
            core_copy(piece, zz, 1, here, here).start()

    def arrive_second(piece, zz):
        here = couple(piece, zz, core, True)
        remote(
            here, here, second_send.at[piece, zz], second_recv.at[piece, zz], across(piece, True)
        ).wait_recv()
        if shared(piece):
            core_copy(piece, zz, 2, here, here).start()

    def each(distance, action):
        if distance == 0:
            action(z, None)
            return

        @pl.when(z - distance >= 0)
        def _():
            action(z - distance, True)

        @pl.when(z + distance < layers)
        def _():
            action(z + distance, False)

    for step in range(layers + 2):
        for piece in pieces:
            if 0 < step < layers:
                each(step, lambda zz, below, piece=piece: arrive_line(piece, zz, below))
            if 0 <= step - 1 < layers:
                each(step - 1, lambda zz, below, piece=piece: arrive_first(piece, zz))
            if 0 <= step - 2 < layers:
                each(step - 2, lambda zz, below, piece=piece: arrive_second(piece, zz))

    heads_out.wait_send()
    tokens_out.wait_send()
    remote(
        token_room, tokens_all.at[1], pair_send.at[1], pair_recv.at[1], partner
    ).wait_recv()
    tokens_keep.wait()
    other = 1 - core
    for piece in pieces:
        for zz in range(layers):
            mine = block(piece, zz, y, x, core)
            theirs = block(piece, zz, y, x, other)
            crossed = block(piece, *first_block(piece, zz), other)
            first_copy(piece, zz, mine).wait_send()
            second_copy(piece, zz).wait_send()
            if shared(piece):
                core_copy(piece, zz, 0, mine, theirs).wait()
                core_copy(piece, zz, 1, mine, crossed).wait()
                both = couple(piece, zz, other, True)
                core_copy(piece, zz, 2, both, both).wait()

            @pl.when(jnp.logical_and(z < layers - 1, zz <= z))
            def _(piece=piece, zz=zz, mine=mine):
                line_copy(piece, zz, mine, z + 1).wait_send()

            @pl.when(jnp.logical_and(z > 0, zz >= z))
            def _(piece=piece, zz=zz, mine=mine):
                line_copy(piece, zz, mine, z - 1).wait_send()


def gather_all(layers, heads, merge, expand, shrink, small, tokens):
    chips = (layers, 2, 2, 2)
    low = jnp.bfloat16
    count = len(GATHERED)
    sems = pltpu.SemaphoreType.DMA
    inputs = (heads, merge, expand, shrink, small)
    return pl.pallas_call(
        functools.partial(gather_kernel, layers),
        out_shape=[
            jax.ShapeDtypeStruct(chips + heads.shape[1:], low),
            *[jax.ShapeDtypeStruct(chips + part.shape, low) for part in inputs[1:]],
            jax.ShapeDtypeStruct((2,) + tokens.shape, low),
        ],
        in_specs=[pl.BlockSpec(memory_space=pltpu.VMEM)] * 5 + [pl.BlockSpec(memory_space=pl.ANY)],
        out_specs=[pl.BlockSpec(memory_space=pl.ANY)] * 6,
        scratch_shapes=[
            pltpu.VMEM(heads.shape, low),
            pltpu.VMEM(tokens.shape, low),
            sems((2,)),
            sems((2,)),
            sems((2 + count,)),
            sems((count, layers, 2)),
            sems((count, layers)),
            sems((count, layers)),
            sems((count, layers)),
            sems((count, layers)),
            sems((count, layers)),
            sems((count, layers, 3)),
            sems((count, layers, 3)),
        ],
        compiler_params=pltpu.CompilerParams(collective_id=0, has_side_effects=True),
        name="gather_all",
    )(*inputs, tokens)


SCATTERED = (
    ("shrink", 0, 768, False),
    ("expand", 0, 3072, True),
    ("heads", 0, 768, False),
    ("heads", 768, 384, True),
    ("merge", 0, 768, True),
)
BITS = 5


def scatter_kernel(
    layers,
    heads_in,
    merge_in,
    expand_in,
    shrink_in,
    small_in,
    heads_out,
    merge_out,
    expand_out,
    shrink_out,
    small_out,
    square_out,
    totals,
    core_rooms,
    first_rooms,
    second_rooms,
    line_rooms,
    heads_last,
    heads_room,
    small_now,
    small_room,
    square_now,
    square_room,
    load_sem,
    core_send,
    core_recv,
    first_send,
    first_recv,
    second_send,
    second_recv,
    line_send,
    line_recv,
    last_send,
    last_recv,
    small_send,
    small_recv,
    square_send,
    square_recv,
):
    z, y, x, core = place()
    partner = device(z, y, x, 1 - core)
    sources = {"heads": heads_in, "merge": merge_in, "expand": expand_in, "shrink": shrink_in}
    results = {"merge": merge_out, "expand": expand_out, "shrink": shrink_out}
    opposite = (
        partner,
        device(z, y, 1 - x, core),
        device(z, 1 - y, x, core),
        device(z + 1 - 2 * (z % 2), y, x, core),
        device((z + 2) % 4, y, x, core),
    )
    greet(layers, opposite[4:])

    pieces = range(len(SCATTERED))
    low, wide = jnp.bfloat16, jnp.float32

    def is_heads(piece):
        return SCATTERED[piece][0] == "heads"

    def y_first(piece):
        return SCATTERED[piece][3]

    def part(piece, zz, plane):
        name, start, width, _ = SCATTERED[piece]
        if name == "heads":
            return sources[name].at[zz, :, :, :, :, pl.ds(start, width)]
        return sources[name].at[zz, :, :, plane]

    def load(piece, zz):
        return pltpu.make_async_copy(
            part(piece, zz, core), totals[piece].at[zz], load_sem.at[piece, zz]
        )

    def core_copy(piece, zz):
        return remote(
            part(piece, zz, 1 - core),
            core_rooms[piece].at[zz],
            core_send.at[piece, zz],
            core_recv.at[piece, zz],
            partner,
        )

    def first_copy(piece, zz):
        if y_first(piece):
            source, to = totals[piece].at[zz, 1 - y], device(z, 1 - y, x, core)
        else:
            source, to = totals[piece].at[zz, :, 1 - x], device(z, y, 1 - x, core)
        return remote(
            source, first_rooms[piece].at[zz], first_send.at[piece, zz], first_recv.at[piece, zz], to
        )

    def second_copy(piece, zz):
        if y_first(piece):
            source, to = totals[piece].at[zz, y, 1 - x], device(z, y, 1 - x, core)
        else:
            source, to = totals[piece].at[zz, 1 - y, x], device(z, 1 - y, x, core)
        return remote(
            source,
            second_rooms[piece].at[zz],
            second_send.at[piece, zz],
            second_recv.at[piece, zz],
            to,
        )

    def line_copy(piece, zz, downward):
        to = z - 1 if downward else z + 1
        return remote(
            totals[piece].at[zz, y, x],
            line_rooms[piece].at[downward, zz],
            line_send.at[piece, zz],
            line_recv.at[piece, downward, zz],
            device(to, y, x, core),
        )

    def add(piece, target, room):
        target[...] = (target[...].astype(wide) + room[...].astype(wide)).astype(low)

    def begin(piece, zz):
        if not is_heads(piece):
            core_copy(piece, zz).start()
        load(piece, zz).start()

    def layer_of(step):
        return jnp.where(step % 2 == 0, step // 2, layers - 1 - step // 2)

    def start_all(step, carry):
        for piece in pieces:
            begin(piece, layer_of(step))
        return carry

    lax.fori_loop(0, layers, start_all, 0)

    def on_first(piece, zz):
        load(piece, zz).wait()
        if not is_heads(piece):
            core_copy(piece, zz).wait_recv()

            def merge_one(index, carry):
                add(
                    piece,
                    totals[piece].at[zz, index // 2, index % 2],
                    core_rooms[piece].at[zz, index // 2, index % 2],
                )
                return carry

            lax.fori_loop(0, 4, merge_one, 0)
        first_copy(piece, zz).start()

    def on_second(piece, zz):
        first_copy(piece, zz).wait_recv()

        def merge_one(index, carry):
            if y_first(piece):
                target = totals[piece].at[zz, y, index]
            else:
                target = totals[piece].at[zz, index, x]
            add(piece, target, first_rooms[piece].at[zz, index])
            return carry

        lax.fori_loop(0, 2, merge_one, 0)
        second_copy(piece, zz).start()

    def on_line(piece, zz):
        second_copy(piece, zz).wait_recv()
        mine = totals[piece].at[zz, y, x]
        add(piece, mine, second_rooms[piece].at[zz])

        @pl.when(zz > z)
        def _():
            @pl.when(z > 0)
            def _():
                line_copy(piece, zz, 0).wait_recv()
                add(piece, mine, line_rooms[piece].at[0, zz])

            line_copy(piece, zz, 0).start()

        @pl.when(zz < z)
        def _():
            @pl.when(z < layers - 1)
            def _():
                line_copy(piece, zz, 1).wait_recv()
                add(piece, mine, line_rooms[piece].at[1, zz])

            line_copy(piece, zz, 1).start()

    def small_copy(bit):
        return remote(
            small_now.at[bit], small_room.at[bit], small_send.at[bit], small_recv.at[bit], opposite[bit]
        )

    small_now[0] = small_in[...]
    small_copy(0).start()

    def step_all(step, carry):
        @pl.when(step < layers)
        def _():
            for piece in pieces:
                on_first(piece, layer_of(step))

        @pl.when(jnp.logical_and(step >= 1, step <= layers))
        def _():
            for piece in pieces:
                on_second(piece, layer_of(step - 1))

        @pl.when(step >= 2)
        def _():
            for piece in pieces:
                on_line(piece, layer_of(step - 2))

        for bit in range(BITS):

            @pl.when(step == bit)
            def _(bit=bit):
                small_copy(bit).wait_recv()
                summed = small_now[bit] + small_room[bit]
                if bit + 1 < BITS:
                    small_now[bit + 1] = summed
                    small_copy(bit + 1).start()
                else:
                    small_out[...] = summed

        return carry

    lax.fori_loop(0, layers + 2, step_all, 0)

    def squares(value):
        rows, columns = value.shape
        by_row = jnp.sum((value * value).reshape(rows // 8, 8, columns), axis=0)
        total = by_row[:, 0:128]
        for start in range(128, columns, 128):
            total = total + by_row[:, start : start + 128]
        return total

    def last_copy(piece):
        _, start, width, _ = SCATTERED[piece]
        return remote(
            heads_last.at[:, pl.ds(start, width)],
            heads_room.at[:, pl.ds(start, width)],
            last_send.at[piece],
            last_recv.at[piece],
            partner,
        )

    square_now[0] = jnp.zeros((8, 128), wide)
    order = sorted(pieces, key=lambda piece: not is_heads(piece))
    for piece in order:
        name, start, width, _ = SCATTERED[piece]
        mine = totals[piece].at[z, y, x]

        @pl.when(z > 0)
        def _(piece=piece, mine=mine):
            line_copy(piece, z, 0).wait_recv()
            add(piece, mine, line_rooms[piece].at[0, z])

        @pl.when(z < layers - 1)
        def _(piece=piece, mine=mine):
            line_copy(piece, z, 1).wait_recv()
            add(piece, mine, line_rooms[piece].at[1, z])

        if is_heads(piece):
            heads_last[:, start : start + width] = mine[1 - core]
            last_copy(piece).start()
            kept = mine[core].astype(wide)
            heads_out[core, :, start : start + width] = kept
        else:
            kept = mine[...].astype(wide)
            results[name][...] = kept
        square_now[0] += squares(kept)
    for piece in pieces:
        if is_heads(piece):
            _, start, width, _ = SCATTERED[piece]
            last_copy(piece).wait_recv()
            theirs = heads_room[:, start : start + width].astype(wide)
            heads_out[1 - core, :, start : start + width] = theirs
            square_now[0] += squares(theirs)

    for bit in range(BITS):
        across = remote(
            square_now.at[bit],
            square_room.at[bit],
            square_send.at[bit],
            square_recv.at[bit],
            opposite[bit],
        )
        across.start()
        across.wait()
        summed = square_now[bit] + square_room[bit]
        if bit + 1 < BITS:
            square_now[bit + 1] = summed
        else:
            square_out[...] = summed

    for bit in range(BITS):
        small_copy(bit).wait_send()

    def settle(zz, carry):
        for piece in pieces:
            if not is_heads(piece):
                core_copy(piece, zz).wait_send()
            first_copy(piece, zz).wait_send()
            second_copy(piece, zz).wait_send()

            @pl.when(zz > z)
            def _(piece=piece):
                line_copy(piece, zz, 0).wait_send()

            @pl.when(zz < z)
            def _(piece=piece):
                line_copy(piece, zz, 1).wait_send()

        return carry

    lax.fori_loop(0, layers, settle, 0)
    for piece in pieces:
        if is_heads(piece):
            last_copy(piece).wait_send()


def scatter_all(layers, heads, merge, expand, shrink, small):
    low, wide = jnp.bfloat16, jnp.float32
    arrays = {"heads": heads, "merge": merge, "expand": expand, "shrink": shrink}
    sems = pltpu.SemaphoreType.DMA

    def rooms(*lead):
        found = []
        for name, _, width, _ in SCATTERED:
            rows = arrays[name].shape[4]
            tail = (2, rows, width) if name == "heads" else (rows, width)
            found.append(pltpu.VMEM(tuple(lead) + tail, low))
        return found

    def core_rooms():
        return [
            pltpu.VMEM((1, 1, 1, 8, 128), low)
            if name == "heads"
            else pltpu.VMEM((layers, 2, 2, arrays[name].shape[4], width), low)
            for name, _, width, _ in SCATTERED
        ]

    count = len(SCATTERED)
    rows, columns = heads.shape[4:]
    return pl.pallas_call(
        functools.partial(scatter_kernel, layers),
        out_shape=[
            jax.ShapeDtypeStruct((2, rows, columns), wide),
            *[jax.ShapeDtypeStruct(part.shape[4:], wide) for part in (merge, expand, shrink)],
            jax.ShapeDtypeStruct(small.shape, wide),
            jax.ShapeDtypeStruct((8, 128), wide),
        ],
        in_specs=[pl.BlockSpec(memory_space=pl.ANY)] * 4 + [pl.BlockSpec(memory_space=pltpu.VMEM)],
        out_specs=[pl.BlockSpec(memory_space=pltpu.VMEM)] * 6,
        scratch_shapes=[
            rooms(layers, 2, 2),
            core_rooms(),
            rooms(layers, 2),
            rooms(layers),
            rooms(2, layers),
            pltpu.VMEM((rows, columns), low),
            pltpu.VMEM((rows, columns), low),
            pltpu.VMEM((BITS,) + small.shape, wide),
            pltpu.VMEM((BITS,) + small.shape, wide),
            pltpu.VMEM((BITS, 8, 128), wide),
            pltpu.VMEM((BITS, 8, 128), wide),
            sems((count, layers)),
            sems((count, layers)),
            sems((count, layers)),
            sems((count, layers)),
            sems((count, layers)),
            sems((count, layers)),
            sems((count, layers)),
            sems((count, layers)),
            sems((count, 2, layers)),
            sems((count,)),
            sems((count,)),
            sems((BITS,)),
            sems((BITS,)),
            sems((BITS,)),
            sems((BITS,)),
        ],
        compiler_params=pltpu.CompilerParams(
            collective_id=1, has_side_effects=True, vmem_limit_bytes=60 * 2**20
        ),
        name="scatter_all",
    )(heads, merge, expand, shrink, small)


FAR = (((1,), (1,)), ((), ()))
NEAR = (((1,), (0,)), ((), ()))


def dot(left, right, dims=NEAR):
    return lax.dot_general(left, right, dims, preferred_element_type=jnp.float32)


def write_bias(bias, seg_key, seg_query):
    @pl.when(pl.program_id(1) == 0)
    def _():
        bias[...] = jnp.where(seg_key[0] == seg_query[0], 0.0, masked_score)


def both_halves(ref):
    halves, rows, length, lanes = ref.shape
    return ref[...].reshape(halves * rows * length, lanes)


def only_head(head, value):
    lane = lax.broadcasted_iota(jnp.int32, value.shape, 1)
    return jnp.where((lane // HEAD_DIM) == head, value, jnp.zeros_like(value))


def softmax_of(keys, query, bias):
    scores = dot(keys, query, FAR) + bias[...]
    unscaled = jnp.exp(scores - jnp.max(scores, axis=0, keepdims=True))
    return unscaled * (1.0 / jnp.sum(unscaled, axis=0, keepdims=True))


def attend_kernel(query_ref, key_ref, value_ref, seg_key, seg_query, out_ref, bias):
    write_bias(bias, seg_key, seg_query)
    query = both_halves(query_ref) * jnp.asarray(HEAD_DIM**-0.5, jnp.bfloat16)
    keys = both_halves(key_ref)
    values = both_halves(value_ref).T
    found = []
    for head in range(2):
        weights = softmax_of(keys, only_head(head, query), bias).astype(jnp.bfloat16)
        found.append(dot(values[head * HEAD_DIM : (head + 1) * HEAD_DIM], weights))
    context = jnp.concatenate(found, axis=0).T.astype(jnp.bfloat16)
    out_ref[...] = context.reshape(out_ref.shape)


def attend_back_kernel(
    query_ref, key_ref, value_ref, upstream_ref, seg_key, seg_query, out_ref, bias
):
    write_bias(bias, seg_key, seg_query)
    scale = HEAD_DIM**-0.5
    query = both_halves(query_ref) * jnp.asarray(scale, jnp.bfloat16)
    keys = both_halves(key_ref)
    values = both_halves(value_ref)
    upstream = both_halves(upstream_ref)
    flipped = keys.T
    found_query, found_key, found_value = [], [], []
    for head in range(2):
        weights = softmax_of(keys, only_head(head, query), bias)
        grad_weights = dot(only_head(head, values), upstream, FAR)
        inner = jnp.sum(weights * grad_weights, axis=0, keepdims=True)
        grad_scores = (weights * (grad_weights - inner)).astype(jnp.bfloat16)
        found_value.append(dot(weights.astype(jnp.bfloat16), upstream))
        found_key.append(dot(grad_scores, query))
        found_query.append(dot(flipped[head * HEAD_DIM : (head + 1) * HEAD_DIM], grad_scores))
    lane = lax.broadcasted_iota(jnp.int32, found_key[0].shape, 1)
    width = out_ref.shape[3] // 3
    block = query_ref.shape
    at = pl.program_id(1) * LANES

    def store(which, value):
        start = pl.multiple_of(at + which * width, LANES)
        out_ref[:, :, :, pl.ds(start, LANES)] = value.astype(jnp.bfloat16).reshape(block)

    store(0, jnp.concatenate(found_query, axis=0).T * scale)
    store(1, jnp.where(lane < HEAD_DIM, found_key[0], found_key[1]))
    store(2, jnp.where(lane < HEAD_DIM, found_value[0], found_value[1]))


LANES = 128


def head_block(length, first):
    return pl.BlockSpec((2, 1, length, LANES), lambda row, pair: (0, row, 0, first + pair))


def attention_specs(rows, length):
    return [
        pl.BlockSpec((1, 2 * length, 1), lambda row, pair: (row, 0, 0)),
        pl.BlockSpec((1, 1, 2 * length), lambda row, pair: (row, 0, 0)),
    ]


def attend(heads, seg_key, seg_query):
    _, rows, length, columns = heads.shape
    width = columns // 3
    pairs = width // LANES
    flops = 4 * rows * width * (2 * length) ** 2
    return pl.pallas_call(
        attend_kernel,
        grid=(rows, pairs),
        out_shape=jax.ShapeDtypeStruct((2, rows, length, width), jnp.bfloat16),
        in_specs=[
            head_block(length, 0),
            head_block(length, pairs),
            head_block(length, 2 * pairs),
            *attention_specs(rows, length),
        ],
        out_specs=head_block(length, 0),
        scratch_shapes=[pltpu.VMEM((2 * length, 2 * length), jnp.float32)],
        cost_estimate=pl.CostEstimate(
            flops=flops, bytes_accessed=8 * heads.size // 3, transcendentals=flops // 256
        ),
        name="attend",
    )(heads, heads, heads, seg_key, seg_query)


def attend_back(heads, upstream, seg_key, seg_query):
    _, rows, length, columns = heads.shape
    width = columns // 3
    pairs = width // LANES
    flops = 10 * rows * width * (2 * length) ** 2
    return pl.pallas_call(
        attend_back_kernel,
        grid=(rows, pairs),
        out_shape=jax.ShapeDtypeStruct(heads.shape, jnp.bfloat16),
        in_specs=[
            head_block(length, 0),
            head_block(length, pairs),
            head_block(length, 2 * pairs),
            head_block(length, 0),
            *attention_specs(rows, length),
        ],
        out_specs=pl.BlockSpec((2, 1, length, columns), lambda row, pair: (0, row, 0, 0)),
        scratch_shapes=[pltpu.VMEM((2 * length, 2 * length), jnp.float32)],
        cost_estimate=pl.CostEstimate(
            flops=flops, bytes_accessed=14 * heads.size // 3, transcendentals=flops // 640
        ),
        name="attend_back",
    )(heads, heads, heads, upstream, seg_key, seg_query)


def normalize(hidden):
    center = hidden - jnp.mean(hidden, axis=-1, keepdims=True)
    inverse_scale = lax.rsqrt(jnp.mean(center * center, axis=-1, keepdims=True) + norm_epsilon)
    return (center * inverse_scale, inverse_scale)


def norm_back(upstream, normed, inverse_scale):
    mean_upstream = jnp.mean(upstream, axis=-1, keepdims=True)
    mean_cross = jnp.mean(upstream * normed, axis=-1, keepdims=True)
    return inverse_scale * (upstream - mean_upstream - normed * mean_cross)


def gelu_value(inputs):
    return 0.5 * inputs * (1.0 + lax.erf(inputs * root_half))


def gelu_slope(inputs):
    return (
        0.5 * (1.0 + lax.erf(inputs * root_half))
        + inputs * jnp.exp(-0.5 * inputs * inputs) * inv_root_tau
    )


def cross_rows(operand_left, operand_right):
    return lax.dot_general(
        operand_left, operand_right, (((0,), (0,)), ((), ())), preferred_element_type=jnp.float32
    )


def cross_cols(operand_left, operand_right):
    return dot(operand_left, operand_right, FAR)


def adamw(weight, moment, square, gradient, factor, step_rate):
    clipped = gradient * factor
    moment_new = decay_first * moment + (1.0 - decay_first) * clipped
    square_new = decay_second * square + (1.0 - decay_second) * clipped * clipped
    corrected = (
        moment_new
        / (1.0 - decay_first**STEP)
        / (jnp.sqrt(square_new / (1.0 - decay_second**STEP)) + adam_epsilon)
    )
    return (weight - step_rate * (corrected + weight_decay * weight), moment_new, square_new)


def swap_cores(value):
    return lax.ppermute(value, "seq", [(0, 1), (1, 0)])


def gather_plain(chips, heads, merge, expand, shrink, small, tokens):
    core = lax.axis_index("seq")

    def full(part):
        return lax.all_gather(part, ("dp", "seq"), axis=0, tiled=False)

    mine = lax.dynamic_index_in_dim(full(heads), core, 1, keepdims=False)
    return [mine, *map(full, (merge, expand, shrink, small)), jnp.stack([tokens, swap_cores(tokens)])]


def scatter_plain(chips, heads, merge, expand, shrink, small):
    def sums(part):
        flat = part.astype(jnp.float32).reshape((-1,) + part.shape[-2:])
        return lax.psum_scatter(flat, ("dp", "seq"), scatter_dimension=0, tiled=False)

    own = heads.astype(jnp.float32).reshape((-1, 2) + heads.shape[-2:])
    own = lax.psum_scatter(own, "dp", scatter_dimension=0, tiled=False)
    own = lax.all_to_all(own, "seq", split_axis=0, concat_axis=0, tiled=True)
    reduced = [own, *map(sums, (merge, expand, shrink))]
    squares = lax.psum(sum(jnp.sum(part * part) for part in reduced), ("dp", "seq"))
    return [*reduced, lax.psum(small, ("dp", "seq")), squares]


def per_device(
    chips,
    layer_input,
    segment_ids,
    cotangent,
    heads_weight,
    heads_first,
    heads_second,
    merge_weight,
    merge_first,
    merge_second,
    expand_weight,
    expand_first,
    expand_second,
    shrink_weight,
    shrink_first,
    shrink_second,
    norm_gains,
    gains_first,
    gains_second,
    branch_bias,
    branch_first,
    branch_second,
    hidden_bias,
    hidden_first,
    hidden_second,
):
    low, wide = jnp.bfloat16, jnp.float32
    core = lax.axis_index("seq")
    index = lax.axis_index("dp") * 2 + core
    row_count, length = layer_input.shape[:2]
    rows = heads_weight.shape[0]
    devices = chips * 2
    hidden_rows = shrink_weight.shape[0]
    half = D // 2
    flat_input = layer_input.reshape(-1, D)
    tokens = flat_input.shape[0]
    kernels = rows % 8 == 0 and chips == 16
    block = (chips // 4, 2, 2, 2) if kernels else (devices,)

    heads_parts = heads_weight.astype(low).reshape(rows, 3, 2, half)
    heads_parts = heads_parts.transpose(2, 0, 1, 3).reshape(2, rows, 3 * half)
    small_rows = -(-rows // 8) * 8 + 8
    small_part = jnp.zeros((small_rows, LANES), wide)
    small_part = small_part.at[:rows, 0:2].set(norm_gains).at[:rows, 2:8].set(branch_bias)
    small_part = small_part.at[small_rows - 8, :hidden_rows].set(hidden_bias).astype(low)
    gather = gather_all if kernels else gather_plain
    heads_all, merge_all, expand_all, shrink_all, small_all, inputs_all = gather(
        chips // 4,
        heads_parts,
        merge_weight.astype(low),
        expand_weight.astype(low),
        shrink_weight.astype(low),
        small_part,
        flat_input,
    )
    heads_low = heads_all.reshape(D, 3 * half)
    merge_low = merge_all.reshape(D, D)
    expand_low = expand_all.reshape(D, -1)
    shrink_low = shrink_all.reshape(-1, D)
    small_all = small_all.reshape(devices, small_rows, LANES).astype(wide)
    vectors = small_all[:, :rows, :8].reshape(D, 8).T
    gain_one, gain_two = vectors[0], vectors[1]
    hidden_full = small_all[:, small_rows - 8, :hidden_rows].reshape(-1)
    heads_bias = jnp.concatenate(
        [
            lax.dynamic_slice(vectors[2], (core * half,), (half,)),
            jnp.zeros((half,), wide),
            lax.dynamic_slice(vectors[3], (core * half,), (half,)),
        ]
    )

    seg_own = lax.dynamic_slice(segment_ids, (0, core * length), (row_count, length))
    seg_other = lax.dynamic_slice(segment_ids, (0, (1 - core) * length), (row_count, length))
    seg_here = jnp.concatenate([seg_own, seg_other], axis=1)
    seg_key, seg_query = seg_here[:, :, None], seg_here[:, None, :]

    inputs_both = inputs_all.reshape(2 * tokens, D)
    projected = (dot(inputs_both, heads_low) + heads_bias).astype(low)
    heads_here = projected.reshape(2, row_count, length, 3 * half)
    context_here = attend(heads_here, seg_key, seg_query).reshape(2, tokens, half)
    context_other = swap_cores(context_here[1])
    first_heads = jnp.where(core == 0, context_here[0], context_other)
    last_heads = jnp.where(core == 0, context_other, context_here[0])
    flat_context = jnp.concatenate([first_heads, last_heads], axis=1)
    attended = dot(flat_context, merge_low) + vectors[4]
    normed_one, inverse_one = normalize(flat_input.astype(wide) + attended)
    first_low = (normed_one * gain_one + vectors[5]).astype(low)
    pre_active = dot(first_low, expand_low) + hidden_full
    active_low = gelu_value(pre_active).astype(low)
    branch_out = dot(active_low, shrink_low) + vectors[6]
    normed_two, inverse_two = normalize(first_low.astype(wide) + branch_out)
    work_output = (normed_two * gain_two + vectors[7]).astype(low).reshape(layer_input.shape)

    upstream = cotangent.reshape(-1, D).astype(wide)
    grad_gain_two = jnp.sum(upstream * normed_two, axis=0)
    grad_shift_two = jnp.sum(upstream, axis=0)
    grad_second = norm_back(upstream * gain_two, normed_two, inverse_two)
    branch_grad = grad_second.astype(low)
    grad_shrink = cross_rows(active_low, branch_grad).astype(low)
    grad_shrink_bias = jnp.sum(branch_grad.astype(wide), axis=0)
    active_grad = (cross_cols(branch_grad, shrink_low) * gelu_slope(pre_active)).astype(low)
    grad_expand = cross_rows(first_low, active_grad).astype(low)
    grad_hidden = jnp.sum(active_grad.astype(wide), axis=0)
    grad_first = grad_second + cross_cols(active_grad, expand_low)
    grad_gain_one = jnp.sum(grad_first * normed_one, axis=0)
    grad_shift_one = jnp.sum(grad_first, axis=0)
    grad_sum_one = norm_back(grad_first * gain_one, normed_one, inverse_one)
    attended_grad = grad_sum_one.astype(low)
    grad_merge = cross_rows(flat_context, attended_grad).astype(low)
    grad_merge_bias = jnp.sum(attended_grad.astype(wide), axis=0)
    context_grad = cross_cols(attended_grad, merge_low).astype(low)
    context_grad_own = jnp.where(core == 0, context_grad[:, :half], context_grad[:, half:])
    context_grad_other = swap_cores(
        jnp.where(core == 0, context_grad[:, half:], context_grad[:, :half])
    )
    grad_here = jnp.stack([context_grad_own, context_grad_other])
    heads_grad = attend_back(
        heads_here, grad_here.reshape(2, row_count, length, half), seg_key, seg_query
    ).reshape(2 * tokens, 3 * half)
    input_parts = cross_cols(heads_grad, heads_low)
    input_other = swap_cores(input_parts[tokens:].astype(low))
    work_gradient = (grad_sum_one + input_parts[:tokens] + input_other.astype(wide)).reshape(
        layer_input.shape
    )
    grad_heads = cross_rows(inputs_both, heads_grad).astype(low)
    heads_bias_grad = jnp.sum(heads_grad.astype(wide), axis=0)

    def own_columns(piece):
        return lax.dynamic_update_slice(jnp.zeros((D,), wide), piece, (core * half,))

    small_grad = jnp.stack(
        [
            grad_gain_one,
            grad_gain_two,
            own_columns(heads_bias_grad[:half]),
            own_columns(heads_bias_grad[2 * half :]),
            grad_merge_bias,
            grad_shift_one,
            grad_shrink_bias,
            grad_shift_two,
        ]
    )
    small_grad = jnp.concatenate([small_grad, grad_hidden.reshape(-1, D)], axis=0)
    small_grad = jnp.pad(small_grad, ((0, -small_grad.shape[0] % 8), (0, 0)))

    scatter = scatter_all if kernels else scatter_plain
    heads_sum, merge_sum, expand_sum, shrink_sum, small_sum, squares = scatter(
        chips // 4,
        grad_heads.reshape(block + (rows, 3 * half)),
        grad_merge.reshape(block + (rows, D)),
        grad_expand.reshape(block + (rows, expand_weight.shape[1])),
        grad_shrink.reshape(block + (hidden_rows, D)),
        small_grad,
    )
    heads_sum = heads_sum.reshape(2, rows, 3, half)
    heads_sum = heads_sum.transpose(1, 2, 0, 3).reshape(rows, 3 * D)
    vector_sum = lax.dynamic_slice(small_sum, (0, index * rows), (8, rows)).T
    hidden_sum = lax.dynamic_slice(
        small_sum[8 : 8 + hidden_rows * devices // D].reshape(-1), (index * hidden_rows,), (hidden_rows,)
    )
    gradient_norm = jnp.sqrt(jnp.sum(squares) + jnp.sum(small_sum * small_sum))
    factor = jnp.minimum(1.0, clip_limit / gradient_norm)
    reduced = (
        heads_sum,
        merge_sum,
        expand_sum,
        shrink_sum,
        vector_sum[:, 0:2],
        vector_sum[:, 2:8],
        hidden_sum,
    )
    states = (
        (heads_weight, heads_first, heads_second, rate_matrix),
        (merge_weight, merge_first, merge_second, rate_matrix),
        (expand_weight, expand_first, expand_second, rate_matrix),
        (shrink_weight, shrink_first, shrink_second, rate_matrix),
        (norm_gains, gains_first, gains_second, rate_vector),
        (branch_bias, branch_first, branch_second, rate_vector),
        (hidden_bias, hidden_first, hidden_second, rate_vector),
    )
    results = [
        adamw(state[0], state[1], state[2], gradient, factor, state[3])
        for state, gradient in zip(states, reduced)
    ]
    return (
        work_output,
        work_gradient,
        gradient_norm,
        *[value for result in results for value in result],
        *[result[0].astype(low) for result in results[:4]],
    )


def solution(mesh):
    matrix, vector = P(("dp", "seq"), None), P(("dp", "seq"))
    tokens = P("dp", "seq", None)
    states = (matrix,) * 18 + (vector,) * 3
    return jax.shard_map(
        functools.partial(per_device, mesh.shape["dp"]),
        mesh=mesh,
        in_specs=(tokens, P("dp", None), tokens) + states,
        out_specs=(tokens, tokens, P()) + states + (matrix,) * 4,
        check_vma=False,
    )
```

time: 1130 us -> 383 us (0.34); the launches traced: 1110 us -> 376 us
  waiting for transfers between devices: 339 us -> 1.32 us
  local copies, waits for them, and re-layouts: 294 us -> 22.6 us
  blocking collectives: 236 us -> 0 us
  Pallas kernels: 0 us -> 226 us
  matrix products: 156 us -> 83.4 us
  other arithmetic: 57.3 us -> 37.3 us
  between operations: 21.6 us -> 4.31 us
    reduce_scatter x4 -> x0, waiting for transfers between devices: 314 us -> none  [the longest x1 139 us: per_device(): lax.psum_scatter(grad_shrink, ('dp', 'seq'), scatter_dimension=0, tiled=T...]
    pallas_call x0 -> x4, Pallas kernels: none -> 226 us  [the longest x1 100 us: scatter_all(): pl.pallas_call(functools.partial(scatter_kernel, layers), out_shape=[jax....]
    dynamic_update_slice x28 -> x2, local copies, waits for them, and re-layouts: 191 us -> 0.02 us  [own_columns(): lax.dynamic_update_slice(jnp.zeros((D,), wide), piece, (core * half,))]
    all_gather x2 -> x0, blocking collectives: 80.2 us -> none  [the longest x1 43.5 us: per_device(): lax.all_gather(branch_bias.astype(jnp.bfloat16), ('dp', 'seq'), axis=0, t...]
    unnamed x2 -> x0, blocking collectives: 78.7 us -> none
    dot_general x36 -> x8, matrix products: 123 us -> 54.1 us  [dot(): lax.dot_general(left, right, dims, preferred_element_type=jnp.float32)]
    psum x1 -> x0, blocking collectives: 39.7 us -> none  [per_device(): squares_total = lax.psum(squares_local, ('dp', 'seq'))]
    all_to_all x7 -> x0, blocking collectives: 37.7 us -> none  [the longest x1 6.34 us: per_device(): lax.all_to_all(grad_query.astype(jnp.bfloat16), 'seq', split_axis=1, conc...]
  transfers between devices with their start and end apart: 9 -> 3, of which waited for: 4 -> 1; matrix products, arithmetic and copies ran while one was open for 38% -> 5% of each run, Pallas kernels for 0% -> 0%
where the time goes in v1:
time: 383 us; the launch traced here: 376 us
  Pallas kernels  226 us (59%)
  matrix products  83.4 us (22%)
  other arithmetic  37.3 us (10%)
  local copies, waits for them, and re-layouts  22.6 us (6%)
  between operations  4.31 us (1%)
    pallas_call x1, Pallas kernels, scatter_all(): pl.pallas_call(functools.partial(scatter_kernel, layers), out_shape=[jax....  100 us
    pallas_call x1, Pallas kernels, gather_all(): pl.pallas_call(functools.partial(gather_kernel, layers), out_shape=[jax.S...  74.7 us
    dot_general x8, matrix products, dot(): lax.dot_general(left, right, dims, preferred_element_type=jnp.float32)  54.1 us
    pallas_call x1, Pallas kernels, attend_back(): pl.pallas_call(attend_back_kernel, grid=(rows, pairs), out_shape=jax.Shap...  31.2 us
    dot_general x4, matrix products, cross_rows(): lax.dot_general(operand_left, operand_right, (((0,), (0,)), ((), ())), pr...  29.2 us
    pallas_call x1, Pallas kernels, attend(): pl.pallas_call(attend_kernel, grid=(rows, pairs), out_shape=jax.ShapeDtyp...  20.1 us
  transfers between devices with their start and end apart: 3, of which 1 were waited for; matrix products, arithmetic and copies ran while one was open for 5% of the time, Pallas kernels for 0%

profile of v1, /device:TPU:0, one launch (start us, length us, event | category | flops | bytes accessed | tf_op | source)
XLA Modules:
  0.0 375.9 jit_solution(13268201705475184736)
XLA Ops:
  5.9 1.6 convert_element_type.107.expand_in
  7.5 1.6 convert_element_type.108.shrink_in
  9.2 1.5 convert_element_type.106.merge_in
  10.7 2.0 dynamic-slice_select_fusion
  12.7 2.0 scatter.11
  16.1 74.7 %gather_all.1 = (bf16[4,2,2,2,24,1152]{5,4,3,2,1,0:T(8,128)(2,1)}, bf16[4,2,2,2,24,768]{5,4,3,2,1,0:T(8,128)(2,1)}, bf16[4,2,2,2,24,3072]{5,4,3,2,1,0:T(8,128)(2...) custom-call(bf16[2,24,1152]{2,1,0:T(8,128)(2,1)} %reshape.290.heads_, ...), custom_call_target="tpu_custom_call" | custom-call | tf_op jit(solution)/shard_map/gather_all/pallas_call | solution.py:330
  94.2 8.8 %add_convert_fusion = bf16[2048,1152]{1,0:T(8,128)(2,1)} fusion(bf16[2048,768]{1,0:T(8,128)(2,1)} %bitcast.102, bf16[768,1152]{1,0:T(8,128)(2,1)} %bitcast.104, f32[1152]{0:T(1024)S(1)} %pad_maximum_fusion.4), kind=kOutput, calls=%fused_computation.11 | convolution fusion | flops 3628597248 | bytes 9638400 | tf_op jit(solution)/shard_map/dot_general | solution.py:760
  103.1 20.1 %attend.1 = bf16[2,4,256,384]{3,2,1,0:T(8,128)(2,1)} custom-call(bf16[2,4,256,1152]{3,2,1,0:T(8,128)(2,1)} %bitcast.71, bf16[2,4,256,1152]{3,2,1,0:T(8,128)(2,1)} %bitcast.72, bf16[2,4,256,1152]{3,2,1,0:T(8,128)(2,1)} %bitcast.73, s32[4,512,1]{2,1,0:T(8,128)} %copy.68.seg_key, s32[4,1,512]{2,1,0:T(1,128)} %broadcast_in_dim.8.seg_query), custom_call_target="tpu_custom_call" | custom-call | flops 1610612736 | bytes 6291456 | tf_op jit(solution)/shard_map/attend/pallas_call | solution.py:850
  123.2 2.5 fusion.42
  129.7 1.6 fusion.45
  132.5 9.1 %multiply_convert_fusion = (bf16[1024,3072]{1,0:T(8,128)(2,1)S(1)}, f32[1024,3072]{1,0:T(8,128)}) fusion(f32[3072]{0:T(1024)S(1)} %add.248, bf16[768,3072]{1,0:T(8,128)(2,1)S(1)} %bitcast.96, f32[1024,768]{1,0:T(8,128)S(1)} %get-tuple-element.149, f32[768]{0:T(1024)S(1)} %get-tuple-element.99, f32[768]{0:T(1024)S(1)} %get-tuple-element.100, ...), kind=kOutput, calls=%fused_computation.8 | convolution fusion | flops 4854644736 | bytes 26765312 | tf_op jit(solution)/shard_map/dot_general | solution.py:760
  141.7 5.5 %fusion.46 = (f32[1024]{0:T(1024)S(1)}, f32[1024,768]{1,0:T(8,128)S(1)}) fusion(f32[768]{0:T(1024)S(1)} %get-tuple-element.98, bf16[1024,3072]{1,0:T(8,128)(2,1)S(1)} %get-tuple-element.150, bf16[3072,768]{1,0:T(8,128)(2,1)S(1)} %bitcast.100, f32[768]{0:T(1024)S(1)} %get-tuple-element.99, f32[768]{0:T(1024)S(1)} %get-tuple-element.100, ...), kind=kOutput, calls=%fused_computation.131 | convolution fusion | flops 4838915072 | bytes 17323008 | tf_op jit(solution)/shard_map/dot_general | solution.py:760
  149.0 2.5 convert_reduce_fusion.3
  151.5 9.8 %convolution_convert_fusion = bf16[3072,768]{1,0:T(8,128)(2,1)} fusion(bf16[1024,3072]{1,0:T(8,128)(2,1)} %copy-done.36, f32[1024,768]{1,0:T(8,128)S(1)} %get-tuple-element.128), kind=kOutput, calls=%fused_computation.12 | convolution fusion | flops 4834983936 | bytes 14155776 | tf_op jit(solution)/shard_map/dot_general | solution.py:918
  161.3 11.7 %convert_reduce_fusion = (f32[3072]{0:T(1024)S(1)}, bf16[1024,3072]{1,0:T(8,128)(2,1)S(1)}) fusion(f32[1024,3072]{1,0:T(8,128)} %get-tuple-element.151, f32[3072]{0:T(1024)S(1)} %add.248, bf16[3072,768]{1,0:T(8,128)(2,1)S(1)} %bitcast.101, f32[1024,768]{1,0:T(8,128)S(1)} %get-tuple-element.128), kind=kOutput, calls=%fused_computation.7 | convolution fusion | flops 4873516032 | bytes 26763264 | tf_op jit(solution)/shard_map/dot_general | solution.py:760
  173.1 6.1 %multiply_reduce_fusion = (f32[768]{0:T(1024)S(1)}, f32[1024]{0:T(1024)S(1)}, f32[1024]{0:T(1024)S(1)}, f32[768]{0:T(1024)S(1)}, f32[1024,768]{1,0:T(8,128)S(1)}) fusion(f32[1024,768]{1,0:T(8,128)S(1)} %get-tuple-element.149, f32[1024]{0:T(1024)S(1)} %add_rsqrt_fusion.1, f32[1024]{0:T(1024)S(1)} %broadcast_multiply_fusion.5, ...), kind=kOutput, calls=%fused_computation.31 | convolution fusion | flops 4839698432 | bytes 20472832 | tf_op jit(solution)/shard_map/dot_general | solution.py:760
  180.3 1.4 convolution_convert_fusion.3
  183.5 8.0 %convolution_convert_fusion.1 = bf16[768,3072]{1,0:T(8,128)(2,1)} fusion(bf16[1024,3072]{1,0:T(8,128)(2,1)S(1)} %bitcast.109, f32[1024,768]{1,0:T(8,128)S(1)} %get-tuple-element.149, f32[768]{0:T(1024)S(1)} %get-tuple-element.99, f32[768]{0:T(1024)S(1)} %get-tuple-element.100, f32[1024]{0:T(1024)S(1)} %add_rsqrt_fusion.1, f32[1024]{0:T(1024)S(1)} %broadcast_multiply_fusion.5), kind=kOutput, calls=%fused_computation.13 | convolution fusion | flops 4838129664 | bytes 14170112 | tf_op jit(solution)/shard_map/dot_general | solution.py:918
  191.6 3.9 %convolution_convert_fusion.4 = bf16[768,768]{1,0:T(8,128)(2,1)} fusion(bf16[1024,384]{1,0:T(8,128)(2,1)} %copy-done.10, bf16[1024,384]{1,0:T(8,128)(2,1)} %copy-done.9, f32[1024,768]{1,0:T(8,128)S(1)} %get-tuple-element.130), kind=kOutput, calls=%fused_computation.47 | convolution fusion | flops 1212481536 | bytes 5898240 | tf_op jit(solution)/shard_map/dot_general | solution.py:918
  195.5 2.5 pad_maximum_fusion.1.upstream_ref
  198.0 31.2 %attend_back.1 = bf16[2,4,256,1152]{3,2,1,0:T(8,128)(2,1)} custom-call(bf16[2,4,256,1152]{3,2,1,0:T(8,128)(2,1)} %bitcast.74, bf16[2,4,256,1152]{3,2,1,0:T(8,128)(2,1)} %bitcast.75, bf16[2,4,256,1152]{3,2,1,0:T(8,128)(2,1)} %bitcast.76, bf16[2,4,256,384]{3,2,1,0:T(8,128)(2,1)} %pad_maximum_fusion.1.upstream_ref, s32[4,512,1]{2,1,0:T(8,128)} %copy.68.seg_key, ...), custom_call_target="tpu_custom_call" | custom-call | flops 4026531840 | bytes 11010048 | tf_op jit(solution)/shard_map/attend_back/pallas_call | solution.py:874
  229.2 3.2 convert_reduce_fusion.1
  232.9 7.4 %convolution_convert_fusion.2 = bf16[768,1152]{1,0:T(8,128)(2,1)} fusion(bf16[2048,768]{1,0:T(8,128)(2,1)} %bitcast.103, bf16[2048,1152]{1,0:T(8,128)(2,1)S(1)} %bitcast.78), kind=kOutput, calls=%fused_computation.14 | convolution fusion | flops 3624763392 | bytes 9633792 | tf_op jit(solution)/shard_map/dot_general | solution.py:918
  241.0 100.2 %scatter_all.1 = (f32[2,24,1152]{2,1,0:T(8,128)}, f32[24,768]{1,0:T(8,128)}, f32[24,3072]{1,0:T(8,128)}, f32[96,768]{1,0:T(8,128)}, f32[16,768]{1,0:T(8,128)}, /*index=5*/f32[8,128]{1,0:T(8,128)}) custom-call(bf16[4,2,2,2,24,1152]{5,4,3,2,1,0:T(8,128)(2,1)} %bitcast.83, bf16[4,2,2,2,24,768]{5,4,3,2,1,0:T(8,128)(2,1)} %bitcast.88, ...), custom_call_target="tpu_custom_call" | custom-call | tf_op jit(solution)/shard_map/scatter_all/pallas_call | solution.py:710
  341.9 1.4 multiply_reduce_fusion.5
  343.4 9.9 %fusion.47 = f32[2048,768]{1,0:T(8,128)} fusion(bf16[2048,1152]{1,0:T(8,128)(2,1)} %bitcast.77, bf16[768,1152]{1,0:T(8,128)(2,1)} %bitcast.105), kind=kOutput, calls=%fused_computation.132 | convolution fusion | flops 3623878656 | bytes 12779520 | tf_op jit(solution)/shard_map/dot_general | solution.py:760
  356.0 1.6 broadcast_multiply_fusion
  357.7 1.7 mul.526
  359.4 1.9 copy.70
  361.3 1.8 mul.528
  363.2 2.2 slice.200
  372.1 2.2 fusion.6
  (160 shorter events, 29.6 us)
Async XLA Ops:
  0.7 91.5 %copy-start.25 = (s32[4,512]{1,0:T(4,128)S(1)}, s32[4,512]{1,0:T(4,128)}, u32[]{:S(2)}) copy-start(s32[4,512]{1,0:T(4,128)} %param.31) | copy-start | bytes 24580
  125.7 2.6 collective-permute-start
  131.3 10.4 %slice-start.2 = ((s8[4718592]{0:T(1024)(128)(4,1)}), s8[4194304]{0:T(1024)(128)(4,1)S(1)}, s32[]{:S(2)}) async-start(s8[4718592]{0:T(1024)(128)(4,1)} %bitcast.98), calls=%async_computation.2 | async-start | bytes 8388608
  132.5 9.2 %slice-start.3 = ((s8[4718592]{0:T(1024)(128)(4,1)}), s8[524288]{0:T(1024)(128)(4,1)S(1)}, s32[]{:S(2)}) async-start(s8[4718592]{0:T(1024)(128)(4,1)} %bitcast.98), calls=%async_computation.3 | async-start | bytes 1048576
  141.7 5.5 %copy-start.36 = (bf16[1024,3072]{1,0:T(8,128)(2,1)}, bf16[1024,3072]{1,0:T(8,128)(2,1)S(1)}, u32[]{:S(2)}) copy-start(bf16[1024,3072]{1,0:T(8,128)(2,1)S(1)} %get-tuple-element.150) | copy-start | bytes 18874372
  173.1 6.1 %copy-start.35 = (bf16[1024,3072]{1,0:T(8,128)(2,1)}, bf16[1024,3072]{1,0:T(8,128)(2,1)S(1)}, u32[]{:S(2)}) copy-start(bf16[1024,3072]{1,0:T(8,128)(2,1)S(1)} %get-tuple-element.156) | copy-start | bytes 18874372
  183.1 12.4 %collective-permute-start.1 = (bf16[1024,384]{1,0:T(8,128)(2,1)}, bf16[1024,384]{1,0:T(8,128)(2,1)}, u32[]{:S(2)}, u32[]{:S(2)}) collective-permute-start(bf16[1024,384]{1,0:T(8,128)(2,1)} %get-tuple-element.133), channel_id=1, source_target_pairs={{0,1},{1,0},{2,3},{3,2},{4,5},{5,4},{6,7},{7,6},{8,9},{9,8},{10,11... | collective-permute-start | bytes 2359304 | tf_op jit(solution)/shard_map/ppermute | solution.py:940
  343.4 9.9 %copy-start.29 = (f32[8,128]{1,0:T(8,128)S(1)}, f32[8,128]{1,0:T(8,128)}, u32[]{:S(2)}) copy-start(f32[8,128]{1,0:T(8,128)} %get-tuple-element.82) | copy-start | bytes 12292
  353.2 12.3 %copy-start.24 = (f32[24,6]{0,1:T(8,128)S(1)}, f32[24,6]{0,1:T(8,128)}, u32[]{:S(2)}) copy-start(f32[24,6]{0,1:T(8,128)} %param.48) | copy-start | bytes 1732
  353.2 12.3 %copy-start.26 = (f32[24,6]{0,1:T(8,128)S(1)}, f32[24,6]{0,1:T(8,128)}, u32[]{:S(2)}) copy-start(f32[24,6]{0,1:T(8,128)} %param.49) | copy-start | bytes 1732
  353.2 12.3 %copy-start.27 = (f32[24,6]{0,1:T(8,128)S(1)}, f32[24,6]{0,1:T(8,128)}, u32[]{:S(2)}) copy-start(f32[24,6]{0,1:T(8,128)} %param.50) | copy-start | bytes 1732
  353.2 12.9 %copy-start.28 = (f32[24,2]{0,1:T(2,128)S(1)}, f32[24,2]{0,1:T(2,128)}, u32[]{:S(2)}) copy-start(f32[24,2]{0,1:T(2,128)} %param.45) | copy-start | bytes 580
  353.2 12.9 %copy-start.31 = (f32[24,2]{0,1:T(2,128)S(1)}, f32[24,2]{0,1:T(2,128)}, u32[]{:S(2)}) copy-start(f32[24,2]{0,1:T(2,128)} %param.46) | copy-start | bytes 580
  353.2 14.2 %copy-start.5 = (f32[96,768]{1,0:T(8,128)S(1)}, f32[96,768]{1,0:T(8,128)}, u32[]{:S(2)}) copy-start(f32[96,768]{1,0:T(8,128)} %param.42) | copy-start | bytes 884740
  359.4 9.2 %copy-start.17 = (f32[24,768]{1,0:T(8,128)S(1)}, f32[24,768]{1,0:T(8,128)}, u32[]{:S(2)}) copy-start(f32[24,768]{1,0:T(8,128)} %param.36) | copy-start | bytes 221188
  361.3 8.1 %copy-start.30 = (f32[96]{0:T(128)S(1)}, f32[96]{0:T(128)}, u32[]{:S(2)}) copy-start(f32[96]{0:T(128)} %param.51) | copy-start | bytes 1156
  363.1 4.4 %copy-start.16 = (f32[96,768]{1,0:T(8,128)S(1)}, f32[96,768]{1,0:T(8,128)}, u32[]{:S(2)}) copy-start(f32[96,768]{1,0:T(8,128)} %get-tuple-element.87) | copy-start | bytes 884740
  363.1 5.5 %copy-start.20 = (f32[24,768]{1,0:T(8,128)S(1)}, f32[24,768]{1,0:T(8,128)}, u32[]{:S(2)}) copy-start(f32[24,768]{1,0:T(8,128)} %param.37) | copy-start | bytes 221188
  363.1 5.5 %copy-start.21 = (f32[24,768]{1,0:T(8,128)S(1)}, f32[24,768]{1,0:T(8,128)}, u32[]{:S(2)}) copy-start(f32[24,768]{1,0:T(8,128)} %param.38) | copy-start | bytes 221188
  363.1 5.5 %copy-start.22 = (f32[24,768]{1,0:T(8,128)S(1)}, f32[24,768]{1,0:T(8,128)}, u32[]{:S(2)}) copy-start(f32[24,768]{1,0:T(8,128)} %get-tuple-element.85) | copy-start | bytes 221188
  363.1 6.2 %copy-start.32 = (f32[96]{0:T(128)S(1)}, f32[96]{0:T(128)}, u32[]{:S(2)}) copy-start(f32[96]{0:T(128)} %param.52) | copy-start | bytes 1156
  363.1 6.2 %copy-start.33 = (f32[96]{0:T(128)S(1)}, f32[96]{0:T(128)}, u32[]{:S(2)}) copy-start(f32[96]{0:T(128)} %param.53) | copy-start | bytes 1156
  363.1 6.8 %copy-start.6 = (f32[24,3072]{1,0:T(8,128)S(1)}, f32[24,3072]{1,0:T(8,128)}, u32[]{:S(2)}) copy-start(f32[24,3072]{1,0:T(8,128)} %param.39) | copy-start | bytes 884740
  363.2 6.8 %copy-start.13 = (f32[24,3072]{1,0:T(8,128)S(1)}, f32[24,3072]{1,0:T(8,128)}, u32[]{:S(2)}) copy-start(f32[24,3072]{1,0:T(8,128)} %param.40) | copy-start | bytes 884740
  363.2 6.8 %copy-start.14 = (f32[24,3072]{1,0:T(8,128)S(1)}, f32[24,3072]{1,0:T(8,128)}, u32[]{:S(2)}) copy-start(f32[24,3072]{1,0:T(8,128)} %param.41) | copy-start | bytes 884740
  363.2 6.8 %copy-start.15 = (f32[24,3072]{1,0:T(8,128)S(1)}, f32[24,3072]{1,0:T(8,128)}, u32[]{:S(2)}) copy-start(f32[24,3072]{1,0:T(8,128)} %get-tuple-element.86) | copy-start | bytes 884740
  363.2 7.9 %copy-start.8 = (f32[24,2304]{1,0:T(8,128)S(1)}, f32[24,2304]{1,0:T(8,128)}, u32[]{:S(2)}) copy-start(f32[24,2304]{1,0:T(8,128)} %param.33) | copy-start | bytes 663556
  363.2 7.9 %copy-start.18 = (f32[24,2304]{1,0:T(8,128)S(1)}, f32[24,2304]{1,0:T(8,128)}, u32[]{:S(2)}) copy-start(f32[24,2304]{1,0:T(8,128)} %param.34) | copy-start | bytes 663556
  363.2 7.9 %copy-start.19 = (f32[24,2304]{1,0:T(8,128)S(1)}, f32[24,2304]{1,0:T(8,128)}, u32[]{:S(2)}) copy-start(f32[24,2304]{1,0:T(8,128)} %param.35) | copy-start | bytes 663556
  365.4 5.7 %copy-start.7 = (f32[24,2304]{1,0:T(8,128)S(1)}, f32[24,2304]{1,0:T(8,128)}, u32[]{:S(2)}) copy-start(f32[24,2304]{1,0:T(8,128)} %mul.528) | copy-start | bytes 663556
  365.4 6.6 %collective-permute-start.2 = (bf16[1024,768]{1,0:T(8,128)(2,1)S(1)}, bf16[1024,768]{1,0:T(8,128)(2,1)S(1)}, u32[]{:S(2)}, u32[]{:S(2)}) collective-permute-start(bf16[1024,768]{1,0:T(8,128)(2,1)S(1)} %slice.200), channel_id=1, source_target_pairs={{0,1},{1,0},{2,3},{3,2},{4,5},{5,4},{6,7},{7,6},{8,9},{9,8},{10,11... | collective-permute-start | bytes 4718600 | tf_op jit(solution)/shard_map/ppermute | solution.py:940
  367.5 4.6 %copy-start.2 = (f32[2048,768]{1,0:T(8,128)S(1)}, f32[2048,768]{1,0:T(8,128)}, u32[]{:S(2)}) copy-start(f32[2048,768]{1,0:T(8,128)} %fusion.47) | copy-start | bytes 18874372
  (14 other events, 41.6 us)
